TPU v7x, 32 devices: a whole 2x2x4 slice. The times are simulated.
32 devices in a mesh: section: 4 (over y, x), tensor: 8 (over z, core).
Axes of the slice: x: 2, y: 2, z: 4, core: 2. Of those that a mesh axis runs over, the one named last changes fastest.
Arguments:
- hidden_last: bfloat16 [512, 6656], P(None, 'tensor'), may hold values from -6 to 6
- labels: int32 [512], replicated, may hold values from 0 to 31999
- head_weight: bfloat16 [6656, 32000], P(None, 'tensor'), may hold values from -0.21875 to 0.21875
- layer_inputs: bfloat16 [4, 512, 6656], P('section', None, 'tensor'), may hold values from -6 to 6
- weights: bfloat16 [4, 6656, 6656], P('section', 'tensor'), may hold values from -0.078125 to 0.078125
- row_state: float32 [4, 6656], P('section', 'tensor'), may hold values from 1.173753e-06 to 0.000498845
- col_state: float32 [4, 6656], P('section'), may hold values from 1e-08 to 1e-06
Outputs:
- loss: float32 [], replicated
- input_grads: bfloat16 [4, 512, 6656], P('section', None, 'tensor')
- new_weights: bfloat16 [4, 6656, 6656], P('section', 'tensor')
- new_row_state: float32 [4, 6656], P('section', 'tensor')
- new_col_state: float32 [4, 6656], P('section')
All inputs are finite; a program needn't handle non-finite values.
Results may differ from a plain program's by a relative error of at most 0.007.
Values may be sent and summed in bfloat16 or wider, within the bound.
A program may use at most 192 MiB of HBM per device.

v0:
```python
import functools

import jax
import jax.numpy as jnp
from jax import lax
from jax.experimental import pallas as pl
from jax.experimental.pallas import tpu as pltpu
from jax.sharding import PartitionSpec as P

decay_rate = 0.9
learn_rate = 0.3
tiny_term = 1e-30


MESH = pl.DeviceIdType.MESH


def chain_kernel(
    sections, tensors, part_ref, loss_ref, w_ref, out_ref, g_ref, total_ref, square_ref,
    acc_ref, loss_buf, send_x, recv_x, send_ring, recv_ring, send_mate, recv_mate, send_loss, recv_loss, head_sem,
):
    section = lax.axis_index("section")
    me = lax.axis_index("tensor")
    chips = tensors // 2
    chip, core = me // 2, me % 2
    right = lax.rem(chip + 1, chips) * 2 + core
    left = lax.rem(chip + chips - 1, chips) * 2 + core
    mate = chip * 2 + 1 - core
    features, lanes = part_ref.shape
    half = features // 2 // 16 * 16
    last = sections - 1
    reach = chips // 2

    def block(share, origin, low, size):
        rows = pl.ds(pl.multiple_of(origin * features + low, 16), size)
        return g_ref.at[rows, pl.ds(pl.multiple_of(share * lanes, lanes), lanes)]

    def span(way, distance):
        if 2 * distance < chips:
            return 0, features
        return (0, half) if way == 0 else (half, features - half)

    def remote(src, dst, send, recv, device):
        return pltpu.make_async_remote_copy(
            src_ref=src, dst_ref=dst, send_sem=send, recv_sem=recv, device_id=device, device_id_type=MESH
        )

    def origin_of(way, distance):
        there = chip - distance if way == 0 else chip + distance
        return lax.rem(there + chips, chips) * 2 + core

    def ring_copy(share, way, distance, origin):
        low, size = span(way, distance)
        where = block(share, origin, low, size)
        slot = (share, way * reach + distance - 1)
        return remote(
            where, where, send_ring.at[slot], recv_ring.at[slot], {"tensor": right if way == 0 else left}
        )

    def mate_copy(share, way, distance, origin):
        low, size = (0, features) if distance == 0 else span(way, distance)
        where = block(share, origin, low, size)
        slot = (share, 0 if distance == 0 else 1 + way * reach + distance - 1)
        return remote(where, where, send_mate.at[slot], recv_mate.at[slot], {"tensor": mate})

    def down_copy(share):
        columns = pl.ds(pl.multiple_of(share * lanes, lanes), lanes)
        below = jnp.maximum(section - 1, 0)
        return remote(
            out_ref.at[:, columns], block(share, me, 0, features),
            send_x.at[share], recv_x.at[share], {"section": below},
        )

    def head_copy():
        return remote(
            part_ref, block(section, me, 0, features), head_sem.at[0], recv_x.at[section], {"section": last}
        )

    def own_copy():
        return pltpu.make_async_copy(part_ref, block(last, me, 0, features), head_sem.at[1])

    def loss_copy(step):
        other = lax.rem(section + step, sections)
        return remote(
            loss_ref, loss_buf.at[step - 1], send_loss.at[step - 1], recv_loss.at[step - 1], {"section": other}
        )

    barrier = pltpu.get_barrier_semaphore()
    greeted = [{"tensor": mate}]
    if reach:
        greeted += [{"tensor": right}, {"tensor": left}]
    greeted += [{"section": lax.rem(section + step, sections)} for step in range(1, sections)]
    for device in greeted:
        pl.semaphore_signal(barrier, inc=1, device_id=device, device_id_type=MESH)
    pl.semaphore_wait(barrier, len(greeted))

    @pl.when(section == last)
    def _():
        own_copy().start()

    @pl.when(section != last)
    def _():
        head_copy().start()

    for step in range(1, sections):
        loss_copy(step).start()

    tile = features // 2 if features > 416 else features
    pair = 2 * features
    split = pair % 128 == 0

    def add_squares():
        def rows_step(index, inner):
            entries = w_ref[pl.ds(pl.multiple_of(index * 16, 16), 16), :].astype(jnp.float32)
            return inner + jnp.sum(jnp.reshape(entries * entries, (2, 8, entries.shape[1])), axis=0)

        width = w_ref.shape[1]
        sums = lax.fori_loop(0, features // 16, rows_step, jnp.zeros((8, width), jnp.float32))
        folded = sums[:, :128]
        for start in range(128, width, 128):
            folded = folded + sums[:, start : start + 128]
        square_ref[...] = folded

    @pl.when(section != last)
    def _():
        add_squares()

    def advance(share, carry):
        @pl.when((section == last) & (share == last))
        def _():
            own_copy().wait()

        @pl.when((section != last) | (share != last))
        def _():
            down_copy(share).wait_recv()

        if reach:
            ring_copy(share, 0, 1, me).start()
            ring_copy(share, 1, 1, me).start()
        mate_copy(share, 0, 0, me).start()
        columns = pl.ds(pl.multiple_of(share * lanes, lanes), lanes)
        other = 1 - 2 * core

        def product_of(owner_chip, first):
            if owner_chip is None:
                depth = slice(None)
            else:
                depth = pl.ds(pl.multiple_of(owner_chip * pair, 128), pair)

            def rows_step(index, inner):
                rows = pl.ds(pl.multiple_of(index * tile, 16), tile)
                product = jnp.dot(w_ref[rows, depth], g_ref[depth, columns], preferred_element_type=jnp.float32)
                acc_ref[rows, :] = product if first else acc_ref[rows, :] + product
                return inner

            lax.fori_loop(0, features // tile, rows_step, 0)

        mate_copy(share, 0, 0, me + other).wait_recv()
        if split:
            product_of(chip, True)
        for distance in range(1, reach + 1):
            for way in (0, 1):
                origin = origin_of(way, distance)
                ring_copy(share, way, distance, origin).wait_recv()
                if distance < reach:
                    ring_copy(share, way, distance + 1, origin).start()
                mate_copy(share, way, distance, origin).start()
            for way in (0, 1):
                mate_copy(share, way, distance, origin_of(way, distance) + other).wait_recv()
                if split and (way == 1 or 2 * distance < chips):
                    product_of(origin_of(way, distance) // 2, False)
        if not split:
            product_of(None, True)
        mine = g_ref[pl.ds(pl.multiple_of(me * features, 16), features), columns]
        out_ref[:, columns] = (mine.astype(jnp.float32) + acc_ref[...]).astype(out_ref.dtype)

        @pl.when(section > 0)
        def _():
            down_copy(share).start()

        return carry

    lax.fori_loop(0, sections, advance, 0)

    @pl.when(section == last)
    def _():
        add_squares()

    total = loss_ref[...]
    for step in range(1, sections):
        loss_copy(step).wait_recv()
        total = total + loss_buf[step - 1]
    total_ref[...] = total

    def finish(share, carry):
        @pl.when(section > 0)
        def _():
            down_copy(share).wait_send()

        if reach:
            ring_copy(share, 0, 1, me).wait_send()
            ring_copy(share, 1, 1, me).wait_send()
        mate_copy(share, 0, 0, me).wait_send()
        for distance in range(1, reach + 1):
            for way in (0, 1):
                origin = origin_of(way, distance)
                if distance < reach:
                    ring_copy(share, way, distance + 1, origin).wait_send()
                mate_copy(share, way, distance, origin).wait_send()
        return carry

    lax.fori_loop(0, sections, finish, 0)
    for step in range(1, sections):
        loss_copy(step).wait_send()

    @pl.when(section != last)
    def _():
        head_copy().wait_send()


def gather_kernel(tensors, x_ref, g_ref, send_ring, recv_ring, send_mate, recv_mate, own_sem):
    me = lax.axis_index("tensor")
    chips = tensors // 2
    chip, core = me // 2, me % 2
    right = lax.rem(chip + 1, chips) * 2 + core
    left = lax.rem(chip + chips - 1, chips) * 2 + core
    mate = chip * 2 + 1 - core
    features = x_ref.shape[0]
    half = features // 2 // 16 * 16
    reach = chips // 2

    barrier = pltpu.get_barrier_semaphore()
    greeted = [mate] + ([right, left] if reach else [])
    for device in greeted:
        pl.semaphore_signal(barrier, inc=1, device_id={"tensor": device}, device_id_type=MESH)
    pl.semaphore_wait(barrier, len(greeted))

    def copy(way, distance, origin, to_mate):
        low, size = 0, features
        if distance and 2 * distance == chips:
            low, size = (0, half) if way == 0 else (half, features - half)
        where = g_ref.at[pl.ds(pl.multiple_of(origin * features + low, 16), size), :]
        own = (distance == 0) if to_mate else (distance == 1)
        slot = 0 if distance == 0 else way * reach + distance - 1 + int(to_mate)
        send, recv = (send_mate, recv_mate) if to_mate else (send_ring, recv_ring)
        target = mate if to_mate else (right if way == 0 else left)
        return pltpu.make_async_remote_copy(
            src_ref=x_ref.at[pl.ds(low, size), :] if own else where, dst_ref=where,
            send_sem=send.at[slot], recv_sem=recv.at[slot],
            device_id={"tensor": target}, device_id_type=MESH,
        )

    def origin_of(way, distance):
        there = chip - distance if way == 0 else chip + distance
        return lax.rem(there + chips, chips) * 2 + core

    sent = []

    def start(*args):
        copy(*args).start()
        sent.append(args)

    own_block = g_ref.at[pl.ds(pl.multiple_of(me * features, 16), features), :]
    keep = pltpu.make_async_copy(x_ref, own_block, own_sem.at[0])
    if reach:
        start(0, 1, me, False)
        start(1, 1, me, False)
    start(0, 0, me, True)
    keep.start()
    for distance in range(1, reach + 1):
        for way in (0, 1):
            origin = origin_of(way, distance)
            copy(way, distance, origin, False).wait_recv()
            if distance < reach:
                start(way, distance + 1, origin, False)
            start(way, distance, origin, True)
    other = 1 - 2 * core
    copy(0, 0, me + other, True).wait_recv()
    for distance in range(1, reach + 1):
        for way in (0, 1):
            copy(way, distance, origin_of(way, distance) + other, True).wait_recv()
    keep.wait()
    for args in sent:
        copy(*args).wait_send()


def gather_rows(x, collective_id):
    tensors = lax.axis_size("tensor")
    ring = max(2 * (tensors // 4), 1)
    vmem = pl.BlockSpec(memory_space=pltpu.VMEM)
    dma = pltpu.SemaphoreType.DMA
    return pl.pallas_call(
        functools.partial(gather_kernel, tensors),
        out_shape=jax.ShapeDtypeStruct((tensors * x.shape[0], x.shape[1]), x.dtype),
        in_specs=[vmem],
        out_specs=vmem,
        scratch_shapes=[dma((ring,)), dma((ring,)), dma((ring + 1,)), dma((ring + 1,)), dma((1,))],
        compiler_params=pltpu.CompilerParams(
            collective_id=collective_id, has_side_effects=True, vmem_limit_bytes=24 * 1024 * 1024
        ),
    )(x)


def scatter_kernel(tensors, x_ref, out_ref, near, stage, far, send_near, recv_near, send_far, recv_far):
    me = lax.axis_index("tensor")
    chips = tensors // 2
    chip, core = me // 2, me % 2
    mate = chip * 2 + 1 - core
    features = out_ref.shape[0]

    barrier = pltpu.get_barrier_semaphore()
    chips_out = [lax.rem(chip + step, chips) for step in range(1, chips)]
    greeted = [mate] + [there * 2 + core for there in chips_out]
    for device in greeted:
        pl.semaphore_signal(barrier, inc=1, device_id={"tensor": device}, device_id_type=MESH)
    pl.semaphore_wait(barrier, len(greeted))

    def rows_of(device):
        return pl.ds(pl.multiple_of(device * features, 16), features)

    def near_copy(there):
        return pltpu.make_async_remote_copy(
            src_ref=x_ref.at[rows_of(there * 2 + 1 - core), :], dst_ref=near.at[there],
            send_sem=send_near.at[there], recv_sem=recv_near.at[there],
            device_id={"tensor": mate}, device_id_type=MESH,
        )

    def far_copy(source, there):
        return pltpu.make_async_remote_copy(
            src_ref=stage.at[there], dst_ref=far.at[source],
            send_sem=send_far.at[there], recv_sem=recv_far.at[source],
            device_id={"tensor": there * 2 + core}, device_id_type=MESH,
        )

    def pair_sum(there):
        near_copy(there).wait_recv()
        mine = x_ref[rows_of(there * 2 + core), :].astype(jnp.float32)
        return mine + near[there].astype(jnp.float32)

    for there in chips_out + [chip]:
        near_copy(there).start()
    for there in chips_out:
        stage[there] = pair_sum(there).astype(stage.dtype)
        far_copy(chip, there).start()
    total = pair_sum(chip)
    for there in chips_out:
        far_copy(there, there).wait_recv()
        total = total + far[there].astype(jnp.float32)
    out_ref[...] = total.astype(out_ref.dtype)
    for there in chips_out + [chip]:
        near_copy(there).wait_send()
    for there in chips_out:
        far_copy(chip, there).wait_send()


def scatter_rows(x, collective_id):
    tensors = lax.axis_size("tensor")
    chips = tensors // 2
    features = x.shape[0] // tensors
    vmem = pl.BlockSpec(memory_space=pltpu.VMEM)
    dma = pltpu.SemaphoreType.DMA
    held = pltpu.VMEM((chips, features, x.shape[1]), x.dtype)
    return pl.pallas_call(
        functools.partial(scatter_kernel, tensors),
        out_shape=jax.ShapeDtypeStruct((features, x.shape[1]), x.dtype),
        in_specs=[vmem],
        out_specs=vmem,
        scratch_shapes=[held, held, held] + [dma((chips,))] * 4,
        compiler_params=pltpu.CompilerParams(
            collective_id=collective_id, has_side_effects=True, vmem_limit_bytes=24 * 1024 * 1024
        ),
    )(x)


def exchange_kernel(tensors, x_ref, out_ref, held, send, recv):
    me = lax.axis_index("tensor")
    barrier = pltpu.get_barrier_semaphore()
    others = [lax.rem(me + step, tensors) for step in range(1, tensors)]
    for other in others:
        pl.semaphore_signal(barrier, inc=1, device_id={"tensor": other}, device_id_type=MESH)
    pl.semaphore_wait(barrier, tensors - 1)

    def copy(source, other):
        return pltpu.make_async_remote_copy(
            src_ref=x_ref, dst_ref=held.at[source], send_sem=send.at[other], recv_sem=recv.at[source],
            device_id={"tensor": other}, device_id_type=MESH,
        )

    for other in others:
        copy(me, other).start()
    held[me] = x_ref[...]
    for other in others:
        copy(other, other).wait_recv()
    out_ref[...] = jnp.sum(held[...], axis=0)
    for other in others:
        copy(me, other).wait_send()


def exchange(x, collective_id):
    tensors = lax.axis_size("tensor")
    vmem = pl.BlockSpec(memory_space=pltpu.VMEM)
    dma = pltpu.SemaphoreType.DMA
    return pl.pallas_call(
        functools.partial(exchange_kernel, tensors),
        out_shape=jax.ShapeDtypeStruct(x.shape, x.dtype),
        in_specs=[vmem],
        out_specs=vmem,
        scratch_shapes=[pltpu.VMEM((tensors,) + x.shape, x.dtype), dma((tensors,)), dma((tensors,))],
        compiler_params=pltpu.CompilerParams(
            collective_id=collective_id, has_side_effects=True, vmem_limit_bytes=24 * 1024 * 1024
        ),
    )(x)


def packed_sum(parts, collective_id):
    flat = jnp.concatenate([jnp.reshape(part, (-1,)) for part in parts])
    rows = -(-flat.shape[0] // 1024) * 8
    flat = jnp.pad(flat, (0, rows * 128 - flat.shape[0])).reshape(rows, 128)
    flat = exchange(flat, collective_id).reshape(-1)
    sums, start = [], 0
    for part in parts:
        sums.append(flat[start : start + part.size].reshape(part.shape))
        start += part.size
    return sums


def chain(part_grad, part_loss, local_weight):
    sections, tensors = lax.axis_size("section"), lax.axis_size("tensor")
    features, lanes = part_grad.shape
    width = features * tensors
    rows = lanes * sections
    ring = max(2 * (tensors // 4), 1)
    dma = pltpu.SemaphoreType.DMA
    vmem = pl.BlockSpec(memory_space=pltpu.VMEM)
    return pl.pallas_call(
        functools.partial(chain_kernel, sections, tensors),
        out_shape=(
            jax.ShapeDtypeStruct((features, rows), jnp.bfloat16),
            jax.ShapeDtypeStruct((width, rows), jnp.bfloat16),
            jax.ShapeDtypeStruct((8, 128), jnp.float32),
            jax.ShapeDtypeStruct((8, 128), jnp.float32),
        ),
        in_specs=[vmem] * 3,
        out_specs=(vmem, vmem, vmem, vmem),
        scratch_shapes=[
            pltpu.VMEM((features, lanes), jnp.float32),
            pltpu.VMEM((max(sections - 1, 1), 8, 128), jnp.float32),
            dma((sections,)),
            dma((sections,)),
            dma((sections, ring)),
            dma((sections, ring)),
            dma((sections, ring + 1)),
            dma((sections, ring + 1)),
            dma((max(sections - 1, 1),)),
            dma((max(sections - 1, 1),)),
            dma((2,)),
        ],
        compiler_params=pltpu.CompilerParams(
            collective_id=0, has_side_effects=True, vmem_limit_bytes=48 * 1024 * 1024
        ),
    )(part_grad, jnp.full((8, 128), part_loss, jnp.float32), local_weight)


def body(hidden_last, labels, head_weight, layer_inputs, weights, row_state, col_state):
    section_count = lax.axis_size("section")
    section_index = lax.axis_index("section")
    all_rows = labels.shape[0]
    model_width = head_weight.shape[0]
    vocab_local = head_weight.shape[1]
    local_weight = weights[0]
    rows_local = local_weight.shape[0]
    saved_all = layer_inputs[0]
    columns = lax.axis_index("tensor") * vocab_local + lax.iota(jnp.int32, vocab_local)
    share_rows = all_rows // section_count
    row_start = section_index * share_rows
    hidden_rows = lax.dynamic_slice_in_dim(hidden_last, row_start, share_rows, 0)
    head_slice = head_weight
    logits = lax.dot_general(
        gather_rows(hidden_rows.T, 3),
        head_slice,
        (((0,), (0,)), ((), ())),
        preferred_element_type=jnp.float32,
    )
    exponent = jnp.exp(logits)
    label_hit = (
        lax.dynamic_slice_in_dim(labels, row_start, share_rows, 0)[:, None] == columns[None, :]
    )
    denominator, picked = packed_sum(
        (
            jnp.sum(exponent, axis=1),
            jnp.sum(jnp.where(label_hit, logits, jnp.zeros_like(logits)), axis=1),
        ),
        1,
    )
    losses = jnp.log(denominator) - picked
    logit_grad = (
        (exponent / denominator[:, None] - label_hit.astype(jnp.float32)) / all_rows
    ).astype(jnp.bfloat16)
    head_slice = head_weight
    part_grad = scatter_rows(
        lax.dot_general(
            head_slice, logit_grad, (((1,), (1,)), ((), ())), preferred_element_type=jnp.float32
        ).astype(jnp.bfloat16),
        4,
    )
    part_loss = jnp.sum(losses)
    outputs, gathered, total, weight_squares = chain(part_grad, part_loss, local_weight)
    loss = total[0, 0] / all_rows
    gradient = lax.dot_general(
        saved_all, gathered, (((0,), (1,)), ((), ())), preferred_element_type=jnp.float32
    )
    weight_float = local_weight.astype(jnp.float32)
    entries = float(model_width * model_width)
    square = gradient * gradient
    squares = square + tiny_term
    row_new = decay_rate * row_state[0] + (1.0 - decay_rate) * jnp.mean(squares, axis=1)
    col_part = jnp.sum(squares, axis=0)
    scaled_part = jnp.sum(square / row_new[:, None], axis=0)
    col_sum, scaled_sum, row_total, weight_total = packed_sum(
        (col_part, scaled_part, jnp.sum(row_new), jnp.sum(weight_squares)), 2
    )
    col_new = decay_rate * col_state[0] + (1.0 - decay_rate) * (col_sum / model_width)
    update_total = row_total * jnp.sum(scaled_sum / col_new)
    factor = (
        learn_rate
        * jnp.sqrt(weight_total / entries)
        / jnp.maximum(1.0, jnp.sqrt(update_total / entries))
    )
    update = gradient * (lax.rsqrt(row_new)[:, None] * (lax.rsqrt(col_new) * jnp.sqrt(row_total))[None, :])
    new_weight = (weight_float - factor * update).astype(jnp.bfloat16)
    return (loss, outputs.T[None], new_weight[None], row_new[None], col_new[None])


def solution(mesh):
    return jax.shard_map(
        body,
        mesh=mesh,
        in_specs=(
            P(None, "tensor"),
            P(),
            P(None, "tensor"),
            P("section", None, "tensor"),
            P("section", "tensor", None),
            P("section", "tensor"),
            P("section", None),
        ),
        out_specs=(
            P(),
            P("section", None, "tensor"),
            P("section", "tensor", None),
            P("section", "tensor"),
            P("section", None),
        ),
        check_vma=False,
    )
```

profile of v0, /device:TPU:1, one launch (start us, length us, event | category | flops | bytes accessed | tf_op | source)
XLA Modules:
  0.0 335.6 jit_solution(7677210455320536761)
XLA Ops:
  0.7 0.8 dynamic_slice.7
  1.5 0.7 multiply_reduce_fusion.2
  2.2 0.8 multiply_reduce_fusion.1
  3.0 1.0 dynamic-slice_bitcast_fusion.x_ref
  4.0 21.2 %shard_map.110 = bf16[6656,128]{1,0:T(8,128)(2,1)S(1)} custom-call(bf16[832,128]{1,0:T(8,128)(2,1)S(1)} %dynamic-slice_bitcast_fusion.x_ref), custom_call_target="tpu_custom_call" | custom-call | tf_op jit(solution)/shard_map/pallas_call | solution.py:292
  25.2 22.1 %exponential_reduce_fusion = (f32[128]{0:T(128)S(1)}, f32[128]{0:T(128)S(1)}, f32[128,4000]{0,1:T(8,128)}) fusion(s32[4000]{0:T(1024)S(1)} %iota_add_fusion, s32[128]{0:T(128)S(1)} %dynamic_slice.7, bf16[6656,4000]{0,1:T(8,128)(2,1)} %param.9, bf16[6656,128]{1,0:T(8,128)(2,1)S(1)} %shard_map.110), kind=kOutput, calls=%fused_computation.18 | convolution fusion | flops 6817792000 | bytes 57017472 | tf_op jit(solution)/shard_map/dot_general | solution.py:478
  47.3 5.7 %shard_map.111 = f32[8,128]{1,0:T(8,128)S(1)} custom-call(f32[8,128]{1,0:T(8,128)S(1)} %fusion.22.x_ref), custom_call_target="tpu_custom_call" | custom-call | tf_op jit(solution)/shard_map/pallas_call | solution.py:403
  53.0 0.6 fusion.23
  53.6 28.3 %fusion.7.x_ref = bf16[6656,128]{1,0:T(8,128)(2,1)S(1)} fusion(bf16[6656,4000]{0,1:T(8,128)(2,1)} %param.9, f32[128,4000]{0,1:T(8,128)} %get-tuple-element.26, f32[128]{0:T(128)S(1)} %slice_bitcast_fusion, s32[128]{0:T(128)S(1)} %dynamic_slice.7, s32[4000]{0:T(1024)S(1)} %iota_add_fusion), kind=kOutput, calls=%fused_computation.11 | convolution fusion | flops 6819667968 | bytes 57016960 | tf_op jit(solution)/shard_map/dot_general | solution.py:501
  81.9 20.0 %shard_map.112.part_ref = bf16[832,128]{1,0:T(8,128)(2,1)S(1)} custom-call(bf16[6656,128]{1,0:T(8,128)(2,1)S(1)} %fusion.7.x_ref), custom_call_target="tpu_custom_call" | custom-call | tf_op jit(solution)/shard_map/pallas_call | solution.py:363
  101.9 0.6 broadcast_in_dim.9.loss_ref
  102.6 171.9 %shard_map.113 = (bf16[832,512]{1,0:T(8,128)(2,1)S(1)}, bf16[6656,512]{1,0:T(8,128)(2,1)}, f32[8,128]{1,0:T(8,128)S(1)}, f32[8,128]{1,0:T(8,128)S(1)}) custom-call(bf16[832,128]{1,0:T(8,128)(2,1)S(1)} %shard_map.112.part_ref, f32[8,128]{1,0:T(8,128)S(1)} %broadcast_in_dim.9.loss_ref, bf16[832,6656]{1,0:T(8,128)(2,1)} %bitcast.71), custom_call_target="tpu_custom_call" | custom-call | tf_op jit(solution)/shard_map/pallas_call | solution.py:435
  274.5 0.6 reduce_sum.88
  276.3 12.5 %fusion.4 = (f32[832]{0:T(1024)S(1)}, f32[6656,832]{0,1:T(8,128)}) fusion(bf16[6656,512]{1,0:T(8,128)(2,1)} %get-tuple-element.11, bf16[1,512,832]{1,2,0:T(8,128)(2,1)S(1)} %copy-done), kind=kOutput, calls=%fused_computation.7 | convolution fusion | flops 5687311360 | bytes 29822208 | tf_op jit(solution)/shard_map/dot_general | solution.py:509
  288.8 0.6 reduce_sum.87
  289.4 0.6 reshape_add_fusion
  290.0 9.7 %divide_reduce_fusion = (f32[6656]{0:T(1024)S(1)}, f32[6656]{0:T(1024)S(1)}) fusion(f32[6656,832]{0,1:T(8,128)} %get-tuple-element.28, f32[832]{0:T(1024)S(1)} %get-tuple-element.18), kind=kLoop, calls=%fused_computation.5 | loop fusion | flops 27675648 | bytes 22207744 | tf_op jit(solution)/shard_map/reduce_sum | solution.py:518
  299.7 1.4 concatenate.7
  301.1 11.9 %shard_map.114 = f32[112,128]{1,0:T(8,128)S(1)} custom-call(f32[112,128]{1,0:T(8,128)S(1)} %pad_bitcast_fusion.x_ref), custom_call_target="tpu_custom_call" | custom-call | tf_op jit(solution)/shard_map/pallas_call | solution.py:403
  313.0 0.6 fusion.20
  313.6 0.6 fusion.28
  317.0 0.7 multiply_reduce_fusion
  317.6 15.9 %fusion.6 = bf16[1,832,6656]{2,1,0:T(8,128)(2,1)} fusion(f32[6656,832]{0,1:T(8,128)} %get-tuple-element.28, f32[6656]{0:T(1024)S(1)} %get-tuple-element.19, f32[832]{0:T(1024)S(1)} %get-tuple-element.17, f32[]{:T(128)S(6)} %div.58, bf16[1,832,6656]{2,1,0:T(8,128)(2,1)} %param.11), kind=kLoop, calls=%fused_computation.9 | loop fusion | flops 33226752 | bytes 44332292 | tf_op jit(solution)/shard_map/broadcast_in_dim | solution.py:531
  333.5 0.9 copy.18
  (14 shorter events, 0.6 us)
Async XLA Ops:
  0.6 275.7 %copy-start = (bf16[1,512,832]{1,2,0:T(8,128)(2,1)S(1)}, bf16[1,512,832]{1,2,0:T(8,128)(2,1)}, u32[]{:S(2)}) copy-start(bf16[1,512,832]{1,2,0:T(8,128)(2,1)} %param.10) | copy-start | bytes 2555908
  276.3 13.1 %copy-start.3 = (f32[1,832]{1,0:T(1,128)S(1)}, f32[1,832]{1,0:T(1,128)}, u32[]{:S(2)}) copy-start(f32[1,832]{1,0:T(1,128)} %param.12) | copy-start | bytes 9988
  290.0 27.0 %copy-start.2 = (f32[1,6656]{1,0:T(1,128)S(1)}, f32[1,6656]{1,0:T(1,128)}, u32[]{:S(2)}) copy-start(f32[1,6656]{1,0:T(1,128)} %param.13) | copy-start | bytes 79876
  317.6 16.8 %copy-start.1 = (bf16[1,512,832]{1,2,0:T(8,128)(2,1)S(1)}, bf16[1,512,832]{1,2,0:T(8,128)(2,1)}, u32[]{:S(2)}) copy-start(bf16[1,512,832]{1,2,0:T(8,128)(2,1)} %param.10) | copy-start | bytes 2555908
where the time goes:
time: 336 us
  Pallas kernels  231 us (69%)
  matrix products  62.9 us (19%)
  other arithmetic  30.8 us (9%)
  local copies, waits for them, and re-layouts  5.84 us (2%)
  between operations  5.3 us (2%)
    pallas_call x1, Pallas kernels, chain(): pl.pallas_call(functools.partial(chain_kernel, sections, tensors), out_sh...  172 us
    dot_general x1, matrix products, body(): lax.dot_general(head_slice, logit_grad, (((1,), (1,)), ((), ())), preferr...  28.3 us
    dot_general x1, matrix products, body(): lax.dot_general(gather_rows(hidden_rows.T, 3), head_slice, (((0,), (0,)),...  22.1 us
    pallas_call x1, Pallas kernels, gather_rows(): pl.pallas_call(functools.partial(gather_kernel, tensors), out_shape=jax.S...  21.2 us
    pallas_call x1, Pallas kernels, scatter_rows(): pl.pallas_call(functools.partial(scatter_kernel, tensors), out_shape=jax....  20 us
    pallas_call x2, Pallas kernels, exchange(): pl.pallas_call(functools.partial(exchange_kernel, tensors), out_shape=jax...  17.6 us
    broadcast_in_dim x1, other arithmetic, body(): new_weight[None]  15.9 us
    dot_general x1, matrix products, body(): lax.dot_general(saved_all, gathered, (((0,), (1,)), ((), ())), preferred_...  12.5 us

commit v1 on v0

v1 whole, which is shorter than its diff:
```python
import functools

import jax
import jax.numpy as jnp
from jax import lax
from jax.experimental import pallas as pl
from jax.experimental.pallas import tpu as pltpu
from jax.sharding import PartitionSpec as P

decay_rate = 0.9
learn_rate = 0.3
tiny_term = 1e-30


MESH = pl.DeviceIdType.MESH


def gather_kernel(tensors, x_ref, g_ref, send_ring, recv_ring, send_mate, recv_mate, own_sem):
    me = lax.axis_index("tensor")
    chips = tensors // 2
    chip, core = me // 2, me % 2
    right = lax.rem(chip + 1, chips) * 2 + core
    left = lax.rem(chip + chips - 1, chips) * 2 + core
    mate = chip * 2 + 1 - core
    features = x_ref.shape[0]
    half = features // 2 // 16 * 16
    reach = chips // 2

    barrier = pltpu.get_barrier_semaphore()
    greeted = [mate] + ([right, left] if reach else [])
    for device in greeted:
        pl.semaphore_signal(barrier, inc=1, device_id={"tensor": device}, device_id_type=MESH)
    pl.semaphore_wait(barrier, len(greeted))

    def copy(way, distance, origin, to_mate):
        low, size = 0, features
        if distance and 2 * distance == chips:
            low, size = (0, half) if way == 0 else (half, features - half)
        where = g_ref.at[pl.ds(pl.multiple_of(origin * features + low, 16), size), :]
        own = (distance == 0) if to_mate else (distance == 1)
        slot = 0 if distance == 0 else way * reach + distance - 1 + int(to_mate)
        send, recv = (send_mate, recv_mate) if to_mate else (send_ring, recv_ring)
        target = mate if to_mate else (right if way == 0 else left)
        return pltpu.make_async_remote_copy(
            src_ref=x_ref.at[pl.ds(low, size), :] if own else where, dst_ref=where,
            send_sem=send.at[slot], recv_sem=recv.at[slot],
            device_id={"tensor": target}, device_id_type=MESH,
        )

    def origin_of(way, distance):
        there = chip - distance if way == 0 else chip + distance
        return lax.rem(there + chips, chips) * 2 + core

    sent = []

    def start(*args):
        copy(*args).start()
        sent.append(args)

    own_block = g_ref.at[pl.ds(pl.multiple_of(me * features, 16), features), :]
    keep = pltpu.make_async_copy(x_ref, own_block, own_sem.at[0])
    if reach:
        start(0, 1, me, False)
        start(1, 1, me, False)
    start(0, 0, me, True)
    keep.start()
    for distance in range(1, reach + 1):
        for way in (0, 1):
            origin = origin_of(way, distance)
            copy(way, distance, origin, False).wait_recv()
            if distance < reach:
                start(way, distance + 1, origin, False)
            start(way, distance, origin, True)
    other = 1 - 2 * core
    copy(0, 0, me + other, True).wait_recv()
    for distance in range(1, reach + 1):
        for way in (0, 1):
            copy(way, distance, origin_of(way, distance) + other, True).wait_recv()
    keep.wait()
    for args in sent:
        copy(*args).wait_send()


def gather_rows(x, collective_id):
    tensors = lax.axis_size("tensor")
    ring = max(2 * (tensors // 4), 1)
    vmem = pl.BlockSpec(memory_space=pltpu.VMEM)
    dma = pltpu.SemaphoreType.DMA
    return pl.pallas_call(
        functools.partial(gather_kernel, tensors),
        out_shape=jax.ShapeDtypeStruct((tensors * x.shape[0], x.shape[1]), x.dtype),
        in_specs=[vmem],
        out_specs=vmem,
        scratch_shapes=[dma((ring,)), dma((ring,)), dma((ring + 1,)), dma((ring + 1,)), dma((1,))],
        compiler_params=pltpu.CompilerParams(
            collective_id=collective_id, has_side_effects=True, vmem_limit_bytes=24 * 1024 * 1024
        ),
    )(x)


def scatter_kernel(tensors, x_ref, out_ref, near, stage, far, send_near, recv_near, send_far, recv_far):
    me = lax.axis_index("tensor")
    chips = tensors // 2
    chip, core = me // 2, me % 2
    mate = chip * 2 + 1 - core
    features = out_ref.shape[0]

    barrier = pltpu.get_barrier_semaphore()
    chips_out = [lax.rem(chip + step, chips) for step in range(1, chips)]
    greeted = [mate] + [there * 2 + core for there in chips_out]
    for device in greeted:
        pl.semaphore_signal(barrier, inc=1, device_id={"tensor": device}, device_id_type=MESH)
    pl.semaphore_wait(barrier, len(greeted))

    def rows_of(device):
        return pl.ds(pl.multiple_of(device * features, 16), features)

    def near_copy(there):
        return pltpu.make_async_remote_copy(
            src_ref=x_ref.at[rows_of(there * 2 + 1 - core), :], dst_ref=near.at[there],
            send_sem=send_near.at[there], recv_sem=recv_near.at[there],
            device_id={"tensor": mate}, device_id_type=MESH,
        )

    def far_copy(source, there):
        return pltpu.make_async_remote_copy(
            src_ref=stage.at[there], dst_ref=far.at[source],
            send_sem=send_far.at[there], recv_sem=recv_far.at[source],
            device_id={"tensor": there * 2 + core}, device_id_type=MESH,
        )

    def pair_sum(there):
        near_copy(there).wait_recv()
        mine = x_ref[rows_of(there * 2 + core), :].astype(jnp.float32)
        return mine + near[there].astype(jnp.float32)

    for there in chips_out + [chip]:
        near_copy(there).start()
    for there in chips_out:
        stage[there] = pair_sum(there).astype(stage.dtype)
        far_copy(chip, there).start()
    total = pair_sum(chip)
    for there in chips_out:
        far_copy(there, there).wait_recv()
        total = total + far[there].astype(jnp.float32)
    out_ref[...] = total.astype(out_ref.dtype)
    for there in chips_out + [chip]:
        near_copy(there).wait_send()
    for there in chips_out:
        far_copy(chip, there).wait_send()


def scatter_rows(x, collective_id):
    tensors = lax.axis_size("tensor")
    chips = tensors // 2
    features = x.shape[0] // tensors
    vmem = pl.BlockSpec(memory_space=pltpu.VMEM)
    dma = pltpu.SemaphoreType.DMA
    held = pltpu.VMEM((chips, features, x.shape[1]), x.dtype)
    return pl.pallas_call(
        functools.partial(scatter_kernel, tensors),
        out_shape=jax.ShapeDtypeStruct((features, x.shape[1]), x.dtype),
        in_specs=[vmem],
        out_specs=vmem,
        scratch_shapes=[held, held, held] + [dma((chips,))] * 4,
        compiler_params=pltpu.CompilerParams(
            collective_id=collective_id, has_side_effects=True, vmem_limit_bytes=24 * 1024 * 1024
        ),
    )(x)


def exchange_kernel(tensors, x_ref, out_ref, held, send, recv):
    me = lax.axis_index("tensor")
    barrier = pltpu.get_barrier_semaphore()
    others = [lax.rem(me + step, tensors) for step in range(1, tensors)]
    for other in others:
        pl.semaphore_signal(barrier, inc=1, device_id={"tensor": other}, device_id_type=MESH)
    pl.semaphore_wait(barrier, tensors - 1)

    def copy(source, other):
        return pltpu.make_async_remote_copy(
            src_ref=x_ref, dst_ref=held.at[source], send_sem=send.at[other], recv_sem=recv.at[source],
            device_id={"tensor": other}, device_id_type=MESH,
        )

    for other in others:
        copy(me, other).start()
    held[me] = x_ref[...]
    for other in others:
        copy(other, other).wait_recv()
    out_ref[...] = jnp.sum(held[...], axis=0)
    for other in others:
        copy(me, other).wait_send()


def exchange(x, collective_id):
    tensors = lax.axis_size("tensor")
    vmem = pl.BlockSpec(memory_space=pltpu.VMEM)
    dma = pltpu.SemaphoreType.DMA
    return pl.pallas_call(
        functools.partial(exchange_kernel, tensors),
        out_shape=jax.ShapeDtypeStruct(x.shape, x.dtype),
        in_specs=[vmem],
        out_specs=vmem,
        scratch_shapes=[pltpu.VMEM((tensors,) + x.shape, x.dtype), dma((tensors,)), dma((tensors,))],
        compiler_params=pltpu.CompilerParams(
            collective_id=collective_id, has_side_effects=True, vmem_limit_bytes=24 * 1024 * 1024
        ),
    )(x)


def packed_sum(parts, collective_id):
    flat = jnp.concatenate([jnp.reshape(part, (-1,)) for part in parts])
    rows = -(-flat.shape[0] // 1024) * 8
    flat = jnp.pad(flat, (0, rows * 128 - flat.shape[0])).reshape(rows, 128)
    flat = exchange(flat, collective_id).reshape(-1)
    sums, start = [], 0
    for part in parts:
        sums.append(flat[start : start + part.size].reshape(part.shape))
        start += part.size
    return sums


def step_kernel(
    sections, tensors, count, pack, part_ref, loss_ref, x_ref, row_ref, col_ref, w_ref,
    out_ref, weight_ref, total_ref, row_out, col_out,
    held, carried, grad, acc_ref, row_acc, row_full, loss_buf, vectors, near, pair_sum, spread, final,
    send_x, recv_x, send_z, recv_z, send_mate, recv_mate, send_loss, recv_loss, local_sem, head_sem,
    send_sum, recv_sum, send_far, recv_far,
):
    section = lax.axis_index("section")
    me = lax.axis_index("tensor")
    chips = tensors // 2
    chip, core = me // 2, me % 2
    mate = chip * 2 + 1 - core
    last = sections - 1
    tokens, width = carried.shape
    features = acc_ref.shape[1]
    size = tokens // count
    per = count // sections
    depth = size // pack
    group = vectors.shape[2]
    used = width // group
    joined = 2 if (2 * features) % 128 == 0 else tensors
    span = joined * features

    def rem(a, b):
        return lax.rem(a, b)

    def share_of(step):
        return (last - step // per) * per + rem(step, per)

    def rows_of(step):
        return pl.ds(pl.multiple_of(share_of(step) * size, size), size)

    def packed_of(step):
        return pl.ds(pl.multiple_of(share_of(step) * depth, depth), depth)

    def remote(src, dst, send, recv, device):
        return pltpu.make_async_remote_copy(
            src_ref=src, dst_ref=dst, send_sem=send, recv_sem=recv, device_id=device, device_id_type=MESH
        )

    def block(device, step):
        return held.at[device, packed_of(step), :]

    def line_copy(step, origin, there):
        where = block(origin * 2 + core, step)
        slot = jnp.where(origin == chip, 0, chips) + there
        return remote(where, where, send_z.at[step, slot], recv_z.at[step, origin], {"tensor": there * 2 + core})

    def mate_copy(step, origin, side):
        where = block(origin * 2 + side, step)
        return remote(where, where, send_mate.at[step, origin], recv_mate.at[step, origin], {"tensor": mate})

    def down_copy(step):
        below = jnp.maximum(section - 1, 0)
        return remote(
            out_ref.at[packed_of(step), :], block(me, step), send_x.at[step], recv_x.at[step], {"section": below}
        )

    def head_copy(index):
        step = (last - section) * per + index
        return remote(
            part_ref.at[pl.ds(index * depth, depth), :], block(me, step),
            head_sem.at[index], recv_x.at[step], {"section": last},
        )

    def own_copy(index):
        return pltpu.make_async_copy(
            part_ref.at[pl.ds(index * depth, depth), :], block(me, index), local_sem.at[index]
        )

    def weight_copy():
        return pltpu.make_async_copy(w_ref, weight_ref, local_sem.at[per])

    def loss_copy(source, there):
        return remote(
            loss_ref, loss_buf.at[source], send_loss.at[there], recv_loss.at[source], {"section": there}
        )

    def origin_of(index):
        if index == 0:
            return chip
        near_side = jnp.where(chip * 2 < chips, -1, 1)
        both = jnp.minimum(chip, chips - 1 - chip)
        paired = index <= 2 * both
        distance = jnp.where(paired, (index + 1) // 2, index - both)
        toward_near = paired & (index % 2 == 0)
        return chip + jnp.where(toward_near, near_side, -near_side) * distance

    barrier = pltpu.get_barrier_semaphore()
    greeted = [{"tensor": mate}]
    greeted += [{"tensor": rem(chip + step, chips) * 2 + core} for step in range(1, chips)]
    greeted += [{"section": rem(section + step, sections)} for step in range(1, sections)]
    weight_copy().start()
    for device in greeted:
        pl.semaphore_signal(barrier, inc=1, device_id=device, device_id_type=MESH)
    pl.semaphore_wait(barrier, len(greeted))

    @pl.when(section == last)
    def _():
        for index in range(per):
            own_copy(index).start()

    @pl.when(section != last)
    def _():
        for index in range(per):
            head_copy(index).start()

    for step in range(1, sections):
        loss_copy(section, rem(section + step, sections)).start()

    is_end = (chip == 0) | (chip == chips - 1)

    def launch(step):
        @pl.when((section == last) & (step < per))
        def _():
            own_copy(jnp.minimum(step, per - 1)).wait()

        @pl.when((section != last) | (step >= per))
        def _():
            down_copy(step).wait_recv()

        @pl.when(is_end)
        def _():
            for index in range(1, chips):
                line_copy(step, chip, jnp.where(chip == 0, chips - index, index - 1)).start()

        if chips > 2:
            @pl.when(jnp.logical_not(is_end))
            def _():
                line_copy(step, chip, chip + 1).start()
                line_copy(step, chip, chip - 1).start()

        mate_copy(step, chip, core).start()

    def forwards(origin):
        onward = jnp.where(origin < chip, chip + 1, chip - 1)
        inner = (origin > 0) & (origin < chips - 1)
        return onward, inner & (onward >= 0) & (onward < chips)

    def assemble(step, first):
        for part in range(pack):
            pieces = []
            for offset in range(joined):
                piece = held[first + offset, packed_of(step), :]
                pieces.append(piece[:, part * features : (part + 1) * features])
            rows = pl.ds(pl.multiple_of(share_of(step) * size + part * depth, depth), depth)
            lanes = pl.ds(pl.multiple_of(first * features, 128), span)
            carried[rows, lanes] = jnp.concatenate(pieces, axis=1)

    def product(step, first, fresh):
        lanes = pl.ds(pl.multiple_of(first * features, 128), span)
        value = lax.dot_general(
            carried[rows_of(step), lanes], weight_ref[:, lanes], (((1,), (1,)), ((), ())),
            preferred_element_type=jnp.float32,
        )
        acc_ref[...] = value if fresh else acc_ref[...] + value

    def finish(step, index):
        origin = origin_of(index)
        mate_copy(step, origin, 1 - core).wait_recv()
        if joined == 2:
            assemble(step, origin * 2)
            product(step, origin * 2, index == 0)
        elif index == chips - 1:
            assemble(step, 0)
            product(step, 0, True)

    launch(0)
    weight_copy().wait()

    def add_squares():
        def rows_step(index, inner):
            entries = weight_ref[pl.ds(pl.multiple_of(index * 16, 16), 16), :].astype(jnp.float32)
            return inner + jnp.sum(jnp.reshape(entries * entries, (2, 8, width)), axis=0)

        sums = lax.fori_loop(0, features // 16, rows_step, jnp.zeros((8, width), jnp.float32))
        folded = sums[:, :128]
        for start in range(128, width, 128):
            folded = folded + sums[:, start : start + 128]
        vectors[1, pl.ds(used + 1, 1), :] = jnp.broadcast_to(jnp.sum(folded, keepdims=True), (1, group))

    vectors[...] = jnp.zeros_like(vectors)

    @pl.when(section != last)
    def _():
        add_squares()

    half = count // 2
    low = tokens // 2
    cut = width // half

    def advance(step, carry):
        for index in range(1, chips):
            if index == chips - 1:
                @pl.when(step + 1 < count)
                def _():
                    launch(jnp.minimum(step + 1, count - 1))

            origin = origin_of(index)
            line_copy(step, origin, chip).wait_recv()
            onward, wanted = forwards(origin)

            @pl.when(wanted)
            def _():
                line_copy(step, origin, jnp.clip(onward, 0, chips - 1)).start()

            mate_copy(step, origin, core).start()
            finish(step, index - 1)
        finish(step, chips - 1)
        sums = jnp.concatenate([acc_ref[part * depth : (part + 1) * depth, :] for part in range(pack)], axis=1)
        mine = held[me, packed_of(step), :].astype(jnp.float32)
        out_ref[packed_of(step), :] = (mine + sums).astype(out_ref.dtype)

        @pl.when(section > 0)
        def _():
            down_copy(step).start()

        @pl.when(step >= half)
        def _():
            lanes = pl.ds(pl.multiple_of((step - half) * cut, 128), cut)
            grad[:, lanes] = jnp.dot(
                x_ref[:, low:], carried[low:, lanes], preferred_element_type=jnp.float32
            )

        return carry

    lax.fori_loop(0, count, advance, 0)

    @pl.when(section == last)
    def _():
        add_squares()

    row_acc[...] = jnp.zeros_like(row_acc)

    def gather_squares(index, carry):
        lanes = pl.ds(pl.multiple_of(index * group, 128), group)
        value = grad[:, lanes] + jnp.dot(
            x_ref[:, :low], carried[:low, lanes], preferred_element_type=jnp.float32
        )
        grad[:, lanes] = value
        squares = value * value + tiny_term
        folded = squares[:, :128]
        for start in range(128, group, 128):
            folded = folded + squares[:, start : start + 128]
        row_acc[...] = row_acc[...] + folded
        vectors[0, pl.ds(index, 1), :] = jnp.sum(squares, axis=0, keepdims=True)
        return carry

    lax.fori_loop(0, used, gather_squares, 0)
    sums = jnp.sum(row_acc[...], axis=1, keepdims=True)
    fresh_row = decay_rate * row_ref[...] + (1.0 - decay_rate) * (sums / width)
    row_out[...] = fresh_row
    vectors[1, pl.ds(used, 1), :] = jnp.broadcast_to(jnp.sum(fresh_row, keepdims=True), (1, group))
    row_full[...] = jnp.broadcast_to(1.0 / fresh_row, row_full.shape)

    def gather_scaled(index, carry):
        scaled = []
        for start in range(0, group, 128):
            value = grad[:, pl.ds(pl.multiple_of(index * group + start, 128), 128)]
            scaled.append(jnp.sum(value * value * row_full[...], axis=0, keepdims=True))
        vectors[1, pl.ds(index, 1), :] = jnp.concatenate(scaled, axis=1)
        return carry

    lax.fori_loop(0, used, gather_scaled, 0)

    def mate_sum():
        return remote(vectors.at[1 - core], near, send_sum.at[0], recv_sum.at[0], {"tensor": mate})

    def far_sum(source, there):
        return remote(
            pair_sum, spread.at[source], send_far.at[there], recv_far.at[source], {"tensor": there * 2 + core}
        )

    def mate_total(side):
        return remote(final.at[side], final.at[side], send_sum.at[1], recv_sum.at[1], {"tensor": mate})

    others = [rem(chip + step, chips) for step in range(1, chips)]
    mate_sum().start()
    mate_sum().wait_recv()
    pair_sum[...] = vectors[core] + near[...]
    for there in others:
        far_sum(chip, there).start()
    spread[chip] = pair_sum[...]
    for there in others:
        far_sum(there, there).wait_recv()
    final[core] = jnp.sum(spread[...], axis=0)
    mate_total(core).start()

    total = None
    for step in range(1, sections):
        other = rem(section + step, sections)
        loss_copy(other, other).wait_recv()
    loss_buf[section] = loss_ref[...]
    total_ref[...] = jnp.sum(loss_buf[...], axis=0)

    mate_total(1 - core).wait_recv()

    entries = float(width * width)
    row_total = final[1, used : used + 1, :][:, :1]
    weight_total = final[1, used + 1 : used + 2, :][:, :1]

    def update_columns(index, inner):
        lanes = pl.ds(pl.multiple_of(index * group, 128), group)
        fresh = decay_rate * col_ref[:, lanes] + (1.0 - decay_rate) * (final[0, pl.ds(index, 1), :] / width)
        col_out[:, lanes] = fresh
        return inner + final[1, pl.ds(index, 1), :] / fresh

    scaled = lax.fori_loop(0, used, update_columns, jnp.zeros((1, group), jnp.float32))
    update_total = row_total * jnp.sum(scaled, axis=1, keepdims=True)
    factor = (
        learn_rate * jnp.sqrt(weight_total / entries)
        / jnp.maximum(1.0, jnp.sqrt(update_total / entries))
    )
    row_full[...] = jnp.broadcast_to(
        lax.rsqrt(row_out[...]) * (factor * jnp.sqrt(row_total)), row_full.shape
    )

    def write_weights(index, carry):
        for start in range(0, group, 128):
            lanes = pl.ds(pl.multiple_of(index * group + start, 128), 128)
            change = grad[:, lanes] * (row_full[...] * lax.rsqrt(col_out[:, lanes]))
            weight_ref[:, lanes] = (weight_ref[:, lanes].astype(jnp.float32) - change).astype(weight_ref.dtype)
        return carry

    lax.fori_loop(0, used, write_weights, 0)

    def drain(step, carry):
        @pl.when(section > 0)
        def _():
            down_copy(step).wait_send()

        @pl.when(is_end)
        def _():
            for index in range(1, chips):
                line_copy(step, chip, jnp.where(chip == 0, chips - index, index - 1)).wait_send()

        if chips > 2:
            @pl.when(jnp.logical_not(is_end))
            def _():
                line_copy(step, chip, chip + 1).wait_send()
                line_copy(step, chip, chip - 1).wait_send()

        mate_copy(step, chip, core).wait_send()
        for index in range(1, chips):
            origin = origin_of(index)
            onward, wanted = forwards(origin)

            @pl.when(wanted)
            def _():
                line_copy(step, origin, jnp.clip(onward, 0, chips - 1)).wait_send()

            mate_copy(step, origin, core).wait_send()
        return carry

    lax.fori_loop(0, count, drain, 0)
    for step in range(1, sections):
        loss_copy(section, rem(section + step, sections)).wait_send()

    @pl.when(section != last)
    def _():
        for index in range(per):
            head_copy(index).wait_send()

    mate_sum().wait_send()
    for there in others:
        far_sum(chip, there).wait_send()
    mate_total(core).wait_send()


def step(part, part_loss, saved, local_weight, row_state, col_state):
    sections, tensors = lax.axis_size("section"), lax.axis_size("tensor")
    features, tokens = saved.shape
    width = features * tensors
    chips = tensors // 2
    count = 2 * sections
    size = tokens // count
    pack = 2 if (2 * features) % 128 == 0 and (size // 2) % 16 == 0 else 1
    group = 512 if width % 512 == 0 else 128
    lines = -(-(width // group + 2) // 8) * 8
    part = part.reshape(count // sections, pack, size // pack, features)
    part = jnp.transpose(part, (0, 2, 1, 3)).reshape(tokens // sections // pack, pack * features)
    dma = pltpu.SemaphoreType.DMA
    vmem = pl.BlockSpec(memory_space=pltpu.VMEM)
    single = pltpu.VMEM((lines, group), jnp.float32)
    outputs, weight, total, row_new, col_new = pl.pallas_call(
        functools.partial(step_kernel, sections, tensors, count, pack),
        out_shape=(
            jax.ShapeDtypeStruct((tokens // pack, pack * features), jnp.bfloat16),
            jax.ShapeDtypeStruct((features, width), jnp.bfloat16),
            jax.ShapeDtypeStruct((8, 128), jnp.float32),
            jax.ShapeDtypeStruct((features, 1), jnp.float32),
            jax.ShapeDtypeStruct((1, width), jnp.float32),
        ),
        in_specs=[vmem] * 5 + [pl.BlockSpec(memory_space=pl.ANY)],
        out_specs=(vmem,) * 5,
        scratch_shapes=[
            pltpu.VMEM((tensors, tokens // pack, pack * features), jnp.bfloat16),
            pltpu.VMEM((tokens, width), jnp.bfloat16),
            pltpu.VMEM((features, width), jnp.float32),
            pltpu.VMEM((size, features), jnp.float32),
            pltpu.VMEM((features, 128), jnp.float32),
            pltpu.VMEM((features, 128), jnp.float32),
            pltpu.VMEM((sections, 8, 128), jnp.float32),
            pltpu.VMEM((2, lines, group), jnp.float32),
            single,
            single,
            pltpu.VMEM((chips, lines, group), jnp.float32),
            pltpu.VMEM((2, lines, group), jnp.float32),
            dma((count,)),
            dma((count,)),
            dma((count, 2 * chips)),
            dma((count, chips)),
            dma((count, chips)),
            dma((count, chips)),
            dma((sections,)),
            dma((sections,)),
            dma((count // sections + 1,)),
            dma((count // sections,)),
            dma((2,)),
            dma((2,)),
            dma((chips,)),
            dma((chips,)),
        ],
        compiler_params=pltpu.CompilerParams(
            collective_id=0, has_side_effects=True, vmem_limit_bytes=62 * 1024 * 1024
        ),
    )(part, jnp.full((8, 128), part_loss, jnp.float32), saved, row_state, col_state, local_weight)
    outputs = outputs.reshape(count, size // pack, pack, features)
    outputs = jnp.transpose(outputs, (0, 2, 1, 3)).reshape(tokens, features)
    return outputs, weight, total, row_new, col_new


def body(hidden_last, labels, head_weight, layer_inputs, weights, row_state, col_state):
    section_count = lax.axis_size("section")
    section_index = lax.axis_index("section")
    all_rows = labels.shape[0]
    vocab_local = head_weight.shape[1]
    local_weight = weights[0]
    saved_all = layer_inputs[0]
    columns = lax.axis_index("tensor") * vocab_local + lax.iota(jnp.int32, vocab_local)
    share_rows = all_rows // section_count
    row_start = section_index * share_rows
    hidden_rows = lax.dynamic_slice_in_dim(hidden_last, row_start, share_rows, 0)
    head_slice = head_weight
    logits = lax.dot_general(
        gather_rows(hidden_rows.T, 3),
        head_slice,
        (((0,), (0,)), ((), ())),
        preferred_element_type=jnp.float32,
    )
    exponent = jnp.exp(logits)
    label_hit = (
        lax.dynamic_slice_in_dim(labels, row_start, share_rows, 0)[:, None] == columns[None, :]
    )
    denominator, picked = packed_sum(
        (
            jnp.sum(exponent, axis=1),
            jnp.sum(jnp.where(label_hit, logits, jnp.zeros_like(logits)), axis=1),
        ),
        1,
    )
    losses = jnp.log(denominator) - picked
    logit_grad = (
        (exponent / denominator[:, None] - label_hit.astype(jnp.float32)) / all_rows
    ).astype(jnp.bfloat16)
    head_slice = head_weight
    part_grad = scatter_rows(
        lax.dot_general(
            head_slice, logit_grad, (((1,), (1,)), ((), ())), preferred_element_type=jnp.float32
        ).astype(jnp.bfloat16),
        4,
    )
    part_loss = jnp.sum(losses)
    outputs, new_weight, total, row_new, col_new = step(
        part_grad.T, part_loss, saved_all.T, local_weight, row_state.reshape(-1, 1), col_state
    )
    loss = total[0, 0] / all_rows
    return (loss, outputs[None], new_weight[None], row_new.reshape(1, -1), col_new)


def solution(mesh):
    return jax.shard_map(
        body,
        mesh=mesh,
        in_specs=(
            P(None, "tensor"),
            P(),
            P(None, "tensor"),
            P("section", None, "tensor"),
            P("section", "tensor", None),
            P("section", "tensor"),
            P("section", None),
        ),
        out_specs=(
            P(),
            P("section", None, "tensor"),
            P("section", "tensor", None),
            P("section", "tensor"),
            P("section", None),
        ),
        check_vma=False,
    )
```

time: 336 us -> 316 us (0.940)
  other arithmetic: 30.8 us -> 1.83 us
  local copies, waits for them, and re-layouts: 5.84 us -> 21.8 us
  matrix products: 62.9 us -> 50.4 us
  Pallas kernels: 231 us -> 239 us
    pallas_call x1, Pallas kernels: 172 us -> 192 us  [step(): pl.pallas_call(functools.partial(step_kernel, sections, tensors, count, p...]
    broadcast_in_dim x1 -> x0, other arithmetic: 15.9 us -> none  [body(): new_weight[None]]
    dot_general x1 -> x0, matrix products: 12.5 us -> none  [body(): lax.dot_general(saved_all, gathered, (((0,), (1,)), ((), ())), preferred_...]
    pallas_call x2 -> x1, Pallas kernels: 17.6 us -> 5.69 us  [exchange(): pl.pallas_call(functools.partial(exchange_kernel, tensors), out_shape=jax...]
    reduce_sum x4 -> x0, other arithmetic: 11.5 us -> none  [the longest x1 9.72 us: body(): scaled_part = jnp.sum(square / row_new[:, None], axis=0)]
    unnamed x9, local copies, waits for them, and re-layouts: 0.93 us -> 12.3 us
    reshape x1 -> x5, local copies, waits for them, and re-layouts: 0.01 us -> 5.85 us  [the longest x2 2.75 us: step(): outputs = outputs.reshape(count, size // pack, pack, features)]
where the time goes in v1:
time: 316 us
  Pallas kernels  239 us (76%)
  matrix products  50.4 us (16%)
  local copies, waits for them, and re-layouts  21.8 us (7%)
    pallas_call x1, Pallas kernels, step(): pl.pallas_call(functools.partial(step_kernel, sections, tensors, count, p...  192 us
    dot_general x1, matrix products, body(): lax.dot_general(head_slice, logit_grad, (((1,), (1,)), ((), ())), preferr...  28.3 us
    dot_general x1, matrix products, body(): lax.dot_general(gather_rows(hidden_rows.T, 3), head_slice, (((0,), (0,)),...  22.1 us
    pallas_call x1, Pallas kernels, gather_rows(): pl.pallas_call(functools.partial(gather_kernel, tensors), out_shape=jax.S...  21.2 us
    pallas_call x1, Pallas kernels, scatter_rows(): pl.pallas_call(functools.partial(scatter_kernel, tensors), out_shape=jax....  20 us
    unnamed x9, local copies, waits for them, and re-layouts  12.3 us

profile of v1, /device:TPU:1, one launch (start us, length us, event | category | flops | bytes accessed | tf_op | source)
XLA Modules:
  0.0 315.7 jit_solution(654319424335529234)
XLA Ops:
  0.6 0.0 copy-start
  0.7 0.8 dynamic_slice.7
  1.5 0.3 copy-done
  1.8 1.6 copy.18.row_ref
  3.5 21.2 %shard_map.110 = bf16[6656,128]{1,0:T(8,128)(2,1)S(1)} custom-call(bf16[832,128]{1,0:T(8,128)(2,1)S(1)} %dynamic-slice_bitcast_fusion.x_ref), custom_call_target="tpu_custom_call" | custom-call | tf_op jit(solution)/shard_map/pallas_call | solution.py:89
  24.7 22.1 %exponential_reduce_fusion = (f32[128]{0:T(128)S(1)}, f32[128]{0:T(128)S(1)}, f32[128,4000]{0,1:T(8,128)}) fusion(s32[4000]{0:T(1024)S(1)} %iota_add_fusion, s32[128]{0:T(128)S(1)} %dynamic_slice.7, bf16[6656,4000]{0,1:T(8,128)(2,1)} %param.9, bf16[6656,128]{1,0:T(8,128)(2,1)S(1)} %shard_map.110), kind=kOutput, calls=%fused_computation.8 | convolution fusion | flops 6817792000 | bytes 57017472 | tf_op jit(solution)/shard_map/dot_general | solution.py:668
  46.8 5.7 %shard_map.111 = f32[8,128]{1,0:T(8,128)S(1)} custom-call(f32[8,128]{1,0:T(8,128)S(1)} %fusion.10.x_ref), custom_call_target="tpu_custom_call" | custom-call | tf_op jit(solution)/shard_map/pallas_call | solution.py:200
  52.5 0.6 fusion.11
  53.1 28.3 %fusion.x_ref = bf16[6656,128]{1,0:T(8,128)(2,1)S(1)} fusion(bf16[6656,4000]{0,1:T(8,128)(2,1)} %param.9, f32[128,4000]{0,1:T(8,128)} %get-tuple-element.22, f32[128]{0:T(128)S(1)} %slice_bitcast_fusion, s32[128]{0:T(128)S(1)} %dynamic_slice.7, s32[4000]{0:T(1024)S(1)} %iota_add_fusion), kind=kOutput, calls=%fused_computation.1 | convolution fusion | flops 6819667968 | bytes 57016960 | tf_op jit(solution)/shard_map/dot_general | solution.py:691
  81.4 20.0 %shard_map.112 = bf16[832,128]{1,0:T(8,128)(2,1)S(1)} custom-call(bf16[6656,128]{1,0:T(8,128)(2,1)S(1)} %fusion.x_ref), custom_call_target="tpu_custom_call" | custom-call | tf_op jit(solution)/shard_map/pallas_call | solution.py:160
  101.4 1.2 broadcast_in_dim.13.loss_ref
  102.6 0.2 copy.16
  102.8 0.2 copy.17
  103.0 0.9 reshape.42.part_ref
  103.8 192.3 %shard_map.113 = (bf16[256,1664]{1,0:T(8,128)(2,1)}, bf16[832,6656]{1,0:T(8,128)(2,1)}, f32[8,128]{1,0:T(8,128)}, f32[832,1]{1,0:T(8,128)}, f32[1,6656]{1,0:T(1,128)}) custom-call(bf16[64,1664]{1,0:T(8,128)(2,1)} %reshape.42.part_ref, f32[8,128]{1,0:T(8,128)} %broadcast_in_dim.13.loss_ref, bf16[832,512]{1,0:T(8,128)(2,1)} %bitcast.36, ...), custom_call_target="tpu_custom_call" | custom-call | tf_op jit(solution)/shard_map/pallas_call | solution.py:608
  296.2 1.2 slice.16
  298.0 1.2 reduce
  299.2 0.6 reshape.45
  299.8 2.6 reshape.44
  302.5 0.1 copy.19
  302.6 1.2 copy.20
  303.8 10.2 %copy.24 = bf16[1,832,6656]{2,1,0:T(8,128)(2,1)} copy(bf16[1,832,6656]{2,1,0:T(8,128)(2,1)} %bitcast.32) | data formatting | bytes 22151168
  314.0 0.0 copy-done.2
  314.0 0.6 copy.25
  (7 shorter events, 0.1 us)
Async XLA Ops:
  0.6 1.2 copy-start
  303.8 10.2 %copy-start.2 = (f32[1,6656]{1,0:T(1,128)S(1)}, f32[1,6656]{1,0:T(1,128)}, u32[]{:S(2)}) copy-start(f32[1,6656]{1,0:T(1,128)} %get-tuple-element.32) | copy-start | bytes 79876
  303.8 10.8 %copy-start.1 = (bf16[512,832]{0,1:T(8,128)(2,1)S(1)}, bf16[512,832]{0,1:T(8,128)(2,1)}, u32[]{:S(2)}) copy-start(bf16[512,832]{0,1:T(8,128)(2,1)} %param.7) | copy-start | bytes 2555908

commit v2 on v1

--- a/solution.py
+++ b/solution.py
@@ -223,10 +223,10 @@
 
 def step_kernel(
     sections, tensors, count, pack, part_ref, loss_ref, x_ref, row_ref, col_ref, w_ref,
-    out_ref, weight_ref, total_ref, row_out, col_out,
-    held, carried, grad, acc_ref, row_acc, row_full, loss_buf, vectors, near, pair_sum, spread, final,
+    out_ref, grad_out, total_ref, row_out, row_scale, col_out, col_scale,
+    weight_ref, stage, held, carried, grad, acc_ref, row_acc, row_full, loss_buf, vectors, near, pair_sum, spread, final,
     send_x, recv_x, send_z, recv_z, send_mate, recv_mate, send_loss, recv_loss, local_sem, head_sem,
-    send_sum, recv_sum, send_far, recv_far,
+    send_sum, recv_sum, send_far, recv_far, stage_sem,
 ):
     section = lax.axis_index("section")
     me = lax.axis_index("tensor")
@@ -414,7 +414,7 @@
 
     def advance(step, carry):
         for index in range(1, chips):
-            if index == chips - 1:
+            if index == min(2, chips - 1):
                 @pl.when(step + 1 < count)
                 def _():
                     launch(jnp.minimum(step + 1, count - 1))
@@ -455,18 +455,35 @@
 
     row_acc[...] = jnp.zeros_like(row_acc)
 
+    def stage_copy(index):
+        lanes = pl.ds(pl.multiple_of(index * group, 128), group)
+        slot = rem(index, 2)
+        return pltpu.make_async_copy(stage.at[slot], grad_out.at[:, lanes], stage_sem.at[slot])
+
     def gather_squares(index, carry):
         lanes = pl.ds(pl.multiple_of(index * group, 128), group)
         value = grad[:, lanes] + jnp.dot(
             x_ref[:, :low], carried[:low, lanes], preferred_element_type=jnp.float32
         )
         grad[:, lanes] = value
-        squares = value * value + tiny_term
-        folded = squares[:, :128]
-        for start in range(128, group, 128):
-            folded = folded + squares[:, start : start + 128]
-        row_acc[...] = row_acc[...] + folded
-        vectors[0, pl.ds(index, 1), :] = jnp.sum(squares, axis=0, keepdims=True)
+
+        @pl.when(index > 1)
+        def _():
+            stage_copy(index - 2).wait()
+
+        slot = rem(index, 2)
+        inner = jnp.zeros((8, group), jnp.float32)
+        for start in range(0, features, 16):
+            entries = grad[start : start + 16, lanes]
+            stage[slot, start : start + 16, :] = entries.astype(stage.dtype)
+            squares = entries * entries + tiny_term
+            folded = squares[:, :128]
+            for lane in range(128, group, 128):
+                folded = folded + squares[:, lane : lane + 128]
+            row_acc[start : start + 16, :] = row_acc[start : start + 16, :] + folded
+            inner = inner + jnp.sum(jnp.reshape(squares, (2, 8, group)), axis=0)
+        vectors[0, pl.ds(index, 1), :] = jnp.sum(inner, axis=0, keepdims=True)
+        stage_copy(index).start()
         return carry
 
     lax.fori_loop(0, used, gather_squares, 0)
@@ -477,11 +494,13 @@
     row_full[...] = jnp.broadcast_to(1.0 / fresh_row, row_full.shape)
 
     def gather_scaled(index, carry):
-        scaled = []
-        for start in range(0, group, 128):
-            value = grad[:, pl.ds(pl.multiple_of(index * group + start, 128), 128)]
-            scaled.append(jnp.sum(value * value * row_full[...], axis=0, keepdims=True))
-        vectors[1, pl.ds(index, 1), :] = jnp.concatenate(scaled, axis=1)
+        lanes = pl.ds(pl.multiple_of(index * group, 128), group)
+        inner = jnp.zeros((8, group), jnp.float32)
+        for start in range(0, features, 16):
+            entries = grad[start : start + 16, lanes]
+            shrink = jnp.concatenate([row_full[start : start + 16, :]] * (group // 128), axis=1)
+            inner = inner + jnp.sum(jnp.reshape(entries * entries * shrink, (2, 8, group)), axis=0)
+        vectors[1, pl.ds(index, 1), :] = jnp.sum(inner, axis=0, keepdims=True)
         return carry
 
     lax.fori_loop(0, used, gather_scaled, 0)
@@ -526,6 +545,7 @@
         lanes = pl.ds(pl.multiple_of(index * group, 128), group)
         fresh = decay_rate * col_ref[:, lanes] + (1.0 - decay_rate) * (final[0, pl.ds(index, 1), :] / width)
         col_out[:, lanes] = fresh
+        col_scale[:, lanes] = lax.rsqrt(fresh)
         return inner + final[1, pl.ds(index, 1), :] / fresh
 
     scaled = lax.fori_loop(0, used, update_columns, jnp.zeros((1, group), jnp.float32))
@@ -534,18 +554,9 @@
         learn_rate * jnp.sqrt(weight_total / entries)
         / jnp.maximum(1.0, jnp.sqrt(update_total / entries))
     )
-    row_full[...] = jnp.broadcast_to(
-        lax.rsqrt(row_out[...]) * (factor * jnp.sqrt(row_total)), row_full.shape
-    )
-
-    def write_weights(index, carry):
-        for start in range(0, group, 128):
-            lanes = pl.ds(pl.multiple_of(index * group + start, 128), 128)
-            change = grad[:, lanes] * (row_full[...] * lax.rsqrt(col_out[:, lanes]))
-            weight_ref[:, lanes] = (weight_ref[:, lanes].astype(jnp.float32) - change).astype(weight_ref.dtype)
-        return carry
-
-    lax.fori_loop(0, used, write_weights, 0)
+    row_scale[...] = lax.rsqrt(row_out[...]) * (factor * jnp.sqrt(row_total))
+    for index in (used - 2, used - 1):
+        stage_copy(index).wait()
 
     def drain(step, carry):
         @pl.when(section > 0)
@@ -588,6 +599,36 @@
     for there in others:
         far_sum(chip, there).wait_send()
     mate_total(core).wait_send()
+
+
+def update_kernel(weight_ref, grad_ref, row_ref, col_ref, out_ref):
+    rows, width = out_ref.shape
+    group = 512 if width % 512 == 0 else 128
+    for start in range(0, rows, 16):
+        scale = jnp.broadcast_to(row_ref[start : start + 16, :], (16, group))
+        for lane in range(0, width, group):
+            change = grad_ref[start : start + 16, lane : lane + group].astype(jnp.float32)
+            change = change * (scale * col_ref[:, lane : lane + group])
+            entries = weight_ref[start : start + 16, lane : lane + group].astype(jnp.float32)
+            out_ref[start : start + 16, lane : lane + group] = (entries - change).astype(out_ref.dtype)
+
+
+def update(weight, grad, row_scale, col_scale):
+    features, width = weight.shape
+    rows = max(size for size in range(16, 65, 16) if features % size == 0)
+    tile = pl.BlockSpec((rows, width), lambda index: (index, 0))
+    return pl.pallas_call(
+        update_kernel,
+        grid=(features // rows,),
+        out_shape=jax.ShapeDtypeStruct((features, width), jnp.bfloat16),
+        in_specs=[
+            tile, tile,
+            pl.BlockSpec((rows, 1), lambda index: (index, 0)),
+            pl.BlockSpec((1, width), lambda index: (0, 0)),
+        ],
+        out_specs=tile,
+        compiler_params=pltpu.CompilerParams(vmem_limit_bytes=16 * 1024 * 1024),
+    )(weight, grad, row_scale, col_scale)
 
 
 def step(part, part_loss, saved, local_weight, row_state, col_state):
@@ -604,19 +645,24 @@
     part = jnp.transpose(part, (0, 2, 1, 3)).reshape(tokens // sections // pack, pack * features)
     dma = pltpu.SemaphoreType.DMA
     vmem = pl.BlockSpec(memory_space=pltpu.VMEM)
+    hbm = pl.BlockSpec(memory_space=pl.ANY)
     single = pltpu.VMEM((lines, group), jnp.float32)
-    outputs, weight, total, row_new, col_new = pl.pallas_call(
+    outputs, grad, total, row_new, row_scale, col_new, col_scale = pl.pallas_call(
         functools.partial(step_kernel, sections, tensors, count, pack),
         out_shape=(
             jax.ShapeDtypeStruct((tokens // pack, pack * features), jnp.bfloat16),
             jax.ShapeDtypeStruct((features, width), jnp.bfloat16),
             jax.ShapeDtypeStruct((8, 128), jnp.float32),
             jax.ShapeDtypeStruct((features, 1), jnp.float32),
+            jax.ShapeDtypeStruct((features, 1), jnp.float32),
+            jax.ShapeDtypeStruct((1, width), jnp.float32),
             jax.ShapeDtypeStruct((1, width), jnp.float32),
         ),
-        in_specs=[vmem] * 5 + [pl.BlockSpec(memory_space=pl.ANY)],
-        out_specs=(vmem,) * 5,
+        in_specs=[vmem] * 5 + [hbm],
+        out_specs=(vmem, hbm) + (vmem,) * 5,
         scratch_shapes=[
+            pltpu.VMEM((features, width), jnp.bfloat16),
+            pltpu.VMEM((2, features, group), jnp.bfloat16),
             pltpu.VMEM((tensors, tokens // pack, pack * features), jnp.bfloat16),
             pltpu.VMEM((tokens, width), jnp.bfloat16),
             pltpu.VMEM((features, width), jnp.float32),
@@ -643,13 +689,15 @@
             dma((2,)),
             dma((chips,)),
             dma((chips,)),
+            dma((2,)),
         ],
         compiler_params=pltpu.CompilerParams(
-            collective_id=0, has_side_effects=True, vmem_limit_bytes=62 * 1024 * 1024
+            collective_id=0, has_side_effects=True, vmem_limit_bytes=57 * 1024 * 1024
         ),
     )(part, jnp.full((8, 128), part_loss, jnp.float32), saved, row_state, col_state, local_weight)
     outputs = outputs.reshape(count, size // pack, pack, features)
     outputs = jnp.transpose(outputs, (0, 2, 1, 3)).reshape(tokens, features)
+    weight = update(local_weight, grad, row_scale, col_scale)
     return outputs, weight, total, row_new, col_new
 
 

time: 316 us -> 298 us (0.943)
  Pallas kernels: 239 us -> 223 us
    pallas_call x1, Pallas kernels: 192 us -> 167 us  [step(): pl.pallas_call(functools.partial(step_kernel, sections, tensors, count, p...]
    pallas_call x0 -> x1, Pallas kernels: none -> 8.96 us  [update(): pl.pallas_call(update_kernel, grid=(features // rows,), out_shape=jax.Sha...]
    unnamed x9 -> x16, local copies, waits for them, and re-layouts: 12.3 us -> 10.5 us
where the time goes in v2:
time: 298 us; the launch traced here: 297 us
  Pallas kernels  223 us (75%)
  matrix products  50.4 us (17%)
  local copies, waits for them, and re-layouts  20 us (7%)
    pallas_call x1, Pallas kernels, step(): pl.pallas_call(functools.partial(step_kernel, sections, tensors, count, p...  167 us
    dot_general x1, matrix products, body(): lax.dot_general(head_slice, logit_grad, (((1,), (1,)), ((), ())), preferr...  28.3 us
    dot_general x1, matrix products, body(): lax.dot_general(gather_rows(hidden_rows.T, 3), head_slice, (((0,), (0,)),...  22.1 us
    pallas_call x1, Pallas kernels, gather_rows(): pl.pallas_call(functools.partial(gather_kernel, tensors), out_shape=jax.S...  21.2 us
    pallas_call x1, Pallas kernels, scatter_rows(): pl.pallas_call(functools.partial(scatter_kernel, tensors), out_shape=jax....  20 us
    unnamed x16, local copies, waits for them, and re-layouts  10.5 us
    pallas_call x1, Pallas kernels, update(): pl.pallas_call(update_kernel, grid=(features // rows,), out_shape=jax.Sha...  8.96 us

profile of v2, /device:TPU:1, one launch (start us, length us, event | category | flops | bytes accessed | tf_op | source)
XLA Modules:
  0.0 297.4 jit_solution(5127308589074874835)
XLA Ops:
  0.7 0.8 dynamic_slice.7
  1.5 0.3 copy-done
  1.8 1.6 copy.18.row_ref
  3.5 21.2 %shard_map.110 = bf16[6656,128]{1,0:T(8,128)(2,1)S(1)} custom-call(bf16[832,128]{1,0:T(8,128)(2,1)S(1)} %dynamic-slice_bitcast_fusion.x_ref), custom_call_target="tpu_custom_call" | custom-call | tf_op jit(solution)/shard_map/pallas_call | solution.py:89
  24.7 22.1 %exponential_reduce_fusion = (f32[128]{0:T(128)S(1)}, f32[128]{0:T(128)S(1)}, f32[128,4000]{0,1:T(8,128)}) fusion(s32[4000]{0:T(1024)S(1)} %iota_add_fusion, s32[128]{0:T(128)S(1)} %dynamic_slice.7, bf16[6656,4000]{0,1:T(8,128)(2,1)} %param.9, bf16[6656,128]{1,0:T(8,128)(2,1)S(1)} %shard_map.110), kind=kOutput, calls=%fused_computation.8 | convolution fusion | flops 6817792000 | bytes 57017472 | tf_op jit(solution)/shard_map/dot_general | solution.py:716
  46.8 5.7 %shard_map.111 = f32[8,128]{1,0:T(8,128)S(1)} custom-call(f32[8,128]{1,0:T(8,128)S(1)} %fusion.10.x_ref), custom_call_target="tpu_custom_call" | custom-call | tf_op jit(solution)/shard_map/pallas_call | solution.py:200
  52.5 0.6 fusion.11
  53.1 28.3 %fusion.x_ref = bf16[6656,128]{1,0:T(8,128)(2,1)S(1)} fusion(bf16[6656,4000]{0,1:T(8,128)(2,1)} %param.9, f32[128,4000]{0,1:T(8,128)} %get-tuple-element.26, f32[128]{0:T(128)S(1)} %slice_bitcast_fusion, s32[128]{0:T(128)S(1)} %dynamic_slice.7, s32[4000]{0:T(1024)S(1)} %iota_add_fusion), kind=kOutput, calls=%fused_computation.1 | convolution fusion | flops 6819667968 | bytes 57016960 | tf_op jit(solution)/shard_map/dot_general | solution.py:739
  81.4 20.0 %shard_map.112 = bf16[832,128]{1,0:T(8,128)(2,1)S(1)} custom-call(bf16[6656,128]{1,0:T(8,128)(2,1)S(1)} %fusion.x_ref), custom_call_target="tpu_custom_call" | custom-call | tf_op jit(solution)/shard_map/pallas_call | solution.py:160
  101.4 1.2 broadcast_in_dim.13.loss_ref
  102.6 0.2 copy.16
  102.8 0.2 copy.17
  103.0 0.9 reshape.42.part_ref
  103.8 166.9 %shard_map.113 = (bf16[256,1664]{1,0:T(8,128)(2,1)}, bf16[832,6656]{1,0:T(8,128)(2,1)}, f32[8,128]{1,0:T(8,128)}, f32[832,1]{1,0:T(8,128)}, f32[832,1]{1,0:T(8,1...) custom-call(bf16[64,1664]{1,0:T(8,128)(2,1)} %reshape.42.part_ref, f32[8,128]{1,0:T(8,128)} %broadcast_in_dim.13.loss_ref, ...), custom_call_target="tpu_custom_call" | custom-call | tf_op jit(solution)/shard_map/pallas_call | solution.py:650
  270.7 1.2 slice.16
  272.6 1.2 reduce
  273.8 0.6 reshape.45
  274.4 2.6 reshape.44
  277.1 0.1 copy.19
  277.2 1.2 copy.20
  278.4 4.1 %copy-done.2 = bf16[1,832,6656]{2,1,0:T(8,128)(2,1)S(1)} copy-done((bf16[1,832,6656]{2,1,0:T(8,128)(2,1)S(1)}, bf16[1,832,6656]{2,1,0:T(8,128)(2,1)}, u32[]{:S(2)}) %copy-start.2) | copy-done | bytes 11075608
  282.6 4.1 %copy-done.3 = bf16[832,6656]{1,0:T(8,128)(2,1)S(1)} copy-done((bf16[832,6656]{1,0:T(8,128)(2,1)S(1)}, bf16[832,6656]{1,0:T(8,128)(2,1)}, u32[]{:S(2)}) %copy-start.3) | copy-done | bytes 11075608
  286.7 9.0 %shard_map.114 = bf16[832,6656]{1,0:T(8,128)(2,1)} custom-call(bf16[832,6656]{1,0:T(8,128)(2,1)S(1)} %bitcast.32, bf16[832,6656]{1,0:T(8,128)(2,1)S(1)} %copy-done.3, f32[832,1]{1,0:T(8,128)S(1)} %copy-done.4, f32[1,6656]{1,0:T(1,128)S(1)} %copy-done.5), custom_call_target="tpu_custom_call" | custom-call | tf_op jit(solution)/shard_map/pallas_call | solution.py:620
  295.7 0.6 copy.23
  (15 shorter events, 0.1 us)
Async XLA Ops:
  0.6 1.2 copy-start
  277.0 1.4 copy-start.4
  277.0 1.4 copy-start.5
  278.4 4.1 %copy-start.2 = (bf16[1,832,6656]{2,1,0:T(8,128)(2,1)S(1)}, bf16[1,832,6656]{2,1,0:T(8,128)(2,1)}, u32[]{:S(2)}) copy-start(bf16[1,832,6656]{2,1,0:T(8,128)(2,1)} %param.11) | copy-start | bytes 33226756
  282.6 4.1 %copy-start.3 = (bf16[832,6656]{1,0:T(8,128)(2,1)S(1)}, bf16[832,6656]{1,0:T(8,128)(2,1)}, u32[]{:S(2)}) copy-start(bf16[832,6656]{1,0:T(8,128)(2,1)} %get-tuple-element.14.grad_ref) | copy-start | bytes 33226756
  286.7 9.0 %copy-start.6 = (f32[1,6656]{1,0:T(1,128)S(1)}, f32[1,6656]{1,0:T(1,128)}, u32[]{:S(2)}) copy-start(f32[1,6656]{1,0:T(1,128)} %get-tuple-element.36) | copy-start | bytes 79876
  286.7 9.6 %copy-start.1 = (bf16[512,832]{0,1:T(8,128)(2,1)S(1)}, bf16[512,832]{0,1:T(8,128)(2,1)}, u32[]{:S(2)}) copy-start(bf16[512,832]{0,1:T(8,128)(2,1)} %param.7) | copy-start | bytes 2555908

commit v3 on v2

--- a/solution.py
+++ b/solution.py
@@ -15,210 +15,322 @@
 MESH = pl.DeviceIdType.MESH
 
 
-def gather_kernel(tensors, x_ref, g_ref, send_ring, recv_ring, send_mate, recv_mate, own_sem):
-    me = lax.axis_index("tensor")
-    chips = tensors // 2
-    chip, core = me // 2, me % 2
-    right = lax.rem(chip + 1, chips) * 2 + core
-    left = lax.rem(chip + chips - 1, chips) * 2 + core
-    mate = chip * 2 + 1 - core
-    features = x_ref.shape[0]
-    half = features // 2 // 16 * 16
-    reach = chips // 2
-
-    barrier = pltpu.get_barrier_semaphore()
-    greeted = [mate] + ([right, left] if reach else [])
-    for device in greeted:
-        pl.semaphore_signal(barrier, inc=1, device_id={"tensor": device}, device_id_type=MESH)
-    pl.semaphore_wait(barrier, len(greeted))
-
-    def copy(way, distance, origin, to_mate):
-        low, size = 0, features
-        if distance and 2 * distance == chips:
-            low, size = (0, half) if way == 0 else (half, features - half)
-        where = g_ref.at[pl.ds(pl.multiple_of(origin * features + low, 16), size), :]
-        own = (distance == 0) if to_mate else (distance == 1)
-        slot = 0 if distance == 0 else way * reach + distance - 1 + int(to_mate)
-        send, recv = (send_mate, recv_mate) if to_mate else (send_ring, recv_ring)
-        target = mate if to_mate else (right if way == 0 else left)
-        return pltpu.make_async_remote_copy(
-            src_ref=x_ref.at[pl.ds(low, size), :] if own else where, dst_ref=where,
-            send_sem=send.at[slot], recv_sem=recv.at[slot],
-            device_id={"tensor": target}, device_id_type=MESH,
-        )
-
-    def origin_of(way, distance):
-        there = chip - distance if way == 0 else chip + distance
-        return lax.rem(there + chips, chips) * 2 + core
-
-    sent = []
-
-    def start(*args):
-        copy(*args).start()
-        sent.append(args)
-
-    own_block = g_ref.at[pl.ds(pl.multiple_of(me * features, 16), features), :]
-    keep = pltpu.make_async_copy(x_ref, own_block, own_sem.at[0])
-    if reach:
-        start(0, 1, me, False)
-        start(1, 1, me, False)
-    start(0, 0, me, True)
-    keep.start()
-    for distance in range(1, reach + 1):
-        for way in (0, 1):
-            origin = origin_of(way, distance)
-            copy(way, distance, origin, False).wait_recv()
-            if distance < reach:
-                start(way, distance + 1, origin, False)
-            start(way, distance, origin, True)
-    other = 1 - 2 * core
-    copy(0, 0, me + other, True).wait_recv()
-    for distance in range(1, reach + 1):
-        for way in (0, 1):
-            copy(way, distance, origin_of(way, distance) + other, True).wait_recv()
-    keep.wait()
-    for args in sent:
-        copy(*args).wait_send()
-
-
-def gather_rows(x, collective_id):
-    tensors = lax.axis_size("tensor")
-    ring = max(2 * (tensors // 4), 1)
-    vmem = pl.BlockSpec(memory_space=pltpu.VMEM)
-    dma = pltpu.SemaphoreType.DMA
-    return pl.pallas_call(
-        functools.partial(gather_kernel, tensors),
-        out_shape=jax.ShapeDtypeStruct((tensors * x.shape[0], x.shape[1]), x.dtype),
-        in_specs=[vmem],
-        out_specs=vmem,
-        scratch_shapes=[dma((ring,)), dma((ring,)), dma((ring + 1,)), dma((ring + 1,)), dma((1,))],
-        compiler_params=pltpu.CompilerParams(
-            collective_id=collective_id, has_side_effects=True, vmem_limit_bytes=24 * 1024 * 1024
-        ),
-    )(x)
-
-
-def scatter_kernel(tensors, x_ref, out_ref, near, stage, far, send_near, recv_near, send_far, recv_far):
+def origin_of(chips, chip, index):
+    if index == 0:
+        return chip
+    near_side = jnp.where(chip * 2 < chips, -1, 1)
+    both = jnp.minimum(chip, chips - 1 - chip)
+    paired = index <= 2 * both
+    distance = jnp.where(paired, (index + 1) // 2, index - both)
+    toward_near = paired & (index % 2 == 0)
+    return chip + jnp.where(toward_near, near_side, -near_side) * distance
+
+
+def onward_of(chips, chip, origin):
+    onward = jnp.where(origin < chip, chip + 1, chip - 1)
+    inner = (origin > 0) & (origin < chips - 1)
+    return onward, inner & (onward >= 0) & (onward < chips)
+
+
+def head_kernel(
+    tensors, pack, per, hidden_ref, labels_ref, w_ref, part_ref, loss_ref,
+    weight, tokens_ref, logits, slopes, mine, near_out, near, far_out, far, own_sums, sums,
+    weight_sem, send_line, recv_line, send_mate, recv_mate, send_sum, recv_sum,
+    send_near, recv_near, send_far, recv_far, local_sem,
+):
+    section = lax.axis_index("section")
     me = lax.axis_index("tensor")
     chips = tensors // 2
     chip, core = me // 2, me % 2
     mate = chip * 2 + 1 - core
-    features = out_ref.shape[0]
-
-    barrier = pltpu.get_barrier_semaphore()
-    chips_out = [lax.rem(chip + step, chips) for step in range(1, chips)]
-    greeted = [mate] + [there * 2 + core for there in chips_out]
-    for device in greeted:
-        pl.semaphore_signal(barrier, inc=1, device_id={"tensor": device}, device_id_type=MESH)
-    pl.semaphore_wait(barrier, len(greeted))
-
-    def rows_of(device):
-        return pl.ds(pl.multiple_of(device * features, 16), features)
-
-    def near_copy(there):
+    vocab, width = weight.shape
+    features = width // tensors
+    share = tokens_ref.shape[1]
+    all_rows = labels_ref.shape[1]
+    joined = 2 if (2 * features) % 128 == 0 else tensors
+    groups = tensors // joined
+    span = joined * features
+    is_end = (chip == 0) | (chip == chips - 1)
+    my_tokens = pl.ds(pl.multiple_of(section * share, 128), share)
+
+    def remote(src, dst, send, recv, device):
         return pltpu.make_async_remote_copy(
-            src_ref=x_ref.at[rows_of(there * 2 + 1 - core), :], dst_ref=near.at[there],
-            send_sem=send_near.at[there], recv_sem=recv_near.at[there],
-            device_id={"tensor": mate}, device_id_type=MESH,
+            src_ref=src, dst_ref=dst, send_sem=send, recv_sem=recv,
+            device_id={"tensor": device}, device_id_type=MESH,
         )
 
-    def far_copy(source, there):
-        return pltpu.make_async_remote_copy(
-            src_ref=stage.at[there], dst_ref=far.at[source],
-            send_sem=send_far.at[there], recv_sem=recv_far.at[source],
-            device_id={"tensor": there * 2 + core}, device_id_type=MESH,
-        )
-
-    def pair_sum(there):
-        near_copy(there).wait_recv()
-        mine = x_ref[rows_of(there * 2 + core), :].astype(jnp.float32)
-        return mine + near[there].astype(jnp.float32)
-
-    for there in chips_out + [chip]:
-        near_copy(there).start()
-    for there in chips_out:
-        stage[there] = pair_sum(there).astype(stage.dtype)
-        far_copy(chip, there).start()
-    total = pair_sum(chip)
-    for there in chips_out:
-        far_copy(there, there).wait_recv()
-        total = total + far[there].astype(jnp.float32)
-    out_ref[...] = total.astype(out_ref.dtype)
-    for there in chips_out + [chip]:
-        near_copy(there).wait_send()
-    for there in chips_out:
-        far_copy(chip, there).wait_send()
-
-
-def scatter_rows(x, collective_id):
-    tensors = lax.axis_size("tensor")
-    chips = tensors // 2
-    features = x.shape[0] // tensors
-    vmem = pl.BlockSpec(memory_space=pltpu.VMEM)
-    dma = pltpu.SemaphoreType.DMA
-    held = pltpu.VMEM((chips, features, x.shape[1]), x.dtype)
-    return pl.pallas_call(
-        functools.partial(scatter_kernel, tensors),
-        out_shape=jax.ShapeDtypeStruct((features, x.shape[1]), x.dtype),
-        in_specs=[vmem],
-        out_specs=vmem,
-        scratch_shapes=[held, held, held] + [dma((chips,))] * 4,
-        compiler_params=pltpu.CompilerParams(
-            collective_id=collective_id, has_side_effects=True, vmem_limit_bytes=24 * 1024 * 1024
-        ),
-    )(x)
-
-
-def exchange_kernel(tensors, x_ref, out_ref, held, send, recv):
-    me = lax.axis_index("tensor")
+    def block(device):
+        return tokens_ref.at[pl.ds(pl.multiple_of(device * features, 16), features), :]
+
+    def line_copy(origin, there):
+        where = block(origin * 2 + core)
+        slot = jnp.where(origin == chip, 0, chips) + there
+        return remote(where, where, send_line.at[slot], recv_line.at[origin], there * 2 + core)
+
+    def mate_copy(origin, side):
+        where = block(origin * 2 + side)
+        return remote(where, where, send_mate.at[origin], recv_mate.at[origin], mate)
+
+    def weight_copy(index):
+        first = origin_of(chips, chip, index) * 2 if joined == 2 else 0
+        lanes = pl.ds(pl.multiple_of(first * features, 128), span)
+        return pltpu.make_async_copy(w_ref.at[:, lanes], weight.at[:, lanes], weight_sem.at[index])
+
+    def own_copy():
+        return pltpu.make_async_copy(hidden_ref.at[:, my_tokens], block(me), local_sem.at[0])
+
+    own_copy().start()
+    for index in range(groups):
+        weight_copy(index).start()
+
     barrier = pltpu.get_barrier_semaphore()
     others = [lax.rem(me + step, tensors) for step in range(1, tensors)]
     for other in others:
         pl.semaphore_signal(barrier, inc=1, device_id={"tensor": other}, device_id_type=MESH)
     pl.semaphore_wait(barrier, tensors - 1)
 
-    def copy(source, other):
-        return pltpu.make_async_remote_copy(
-            src_ref=x_ref, dst_ref=held.at[source], send_sem=send.at[other], recv_sem=recv.at[source],
-            device_id={"tensor": other}, device_id_type=MESH,
-        )
+    own_copy().wait()
+
+    @pl.when(is_end)
+    def _():
+        for index in range(1, chips):
+            line_copy(chip, jnp.where(chip == 0, index, chips - 1 - index)).start()
+
+    if chips > 2:
+        @pl.when(jnp.logical_not(is_end))
+        def _():
+            line_copy(chip, chip + 1).start()
+            line_copy(chip, chip - 1).start()
+
+    mate_copy(chip, core).start()
+
+    tile = max([size for size in range(16, 801, 16) if vocab % size == 0], default=vocab)
+
+    def product(index, fresh):
+        first = origin_of(chips, chip, index) * 2 if joined == 2 else 0
+        lanes = pl.ds(pl.multiple_of(first * features, 128), span)
+
+        def rows_step(number, carry):
+            rows = pl.ds(pl.multiple_of(number * tile, 8), tile)
+            value = jnp.dot(weight[rows, lanes], tokens_ref[lanes, :], preferred_element_type=jnp.float32)
+            logits[rows, :] = value if fresh else logits[rows, :] + value
+            return carry
+
+        lax.fori_loop(0, vocab // tile, rows_step, 0)
+
+    for index in range(chips):
+        origin = origin_of(chips, chip, index)
+        if index:
+            line_copy(origin, chip).wait_recv()
+            onward, wanted = onward_of(chips, chip, origin)
+
+            @pl.when(wanted)
+            def _():
+                line_copy(origin, jnp.clip(onward, 0, chips - 1)).start()
+
+            mate_copy(origin, core).start()
+        mate_copy(origin, 1 - core).wait_recv()
+        if joined == 2:
+            weight_copy(index).wait()
+            product(index, index == 0)
+        elif index == chips - 1:
+            weight_copy(0).wait()
+            product(0, True)
+
+    labels = labels_ref[:, my_tokens]
+    step_rows = max(size for size in range(8, 201, 8) if vocab % size == 0)
+
+    def sum_step(number, carry):
+        total, picked = carry
+        rows = pl.ds(pl.multiple_of(number * step_rows, 8), step_rows)
+        value = logits[rows, :]
+        entries = lax.broadcasted_iota(jnp.int32, value.shape, 0) + (me * vocab + number * step_rows)
+        exponent = jnp.exp(value)
+        logits[rows, :] = exponent
+        chosen = jnp.where(entries == labels, value, jnp.zeros_like(value))
+        shape = (step_rows // 8, 8, share)
+        return total + jnp.sum(exponent.reshape(shape), axis=0), picked + jnp.sum(chosen.reshape(shape), axis=0)
+
+    zeros = jnp.zeros((8, share), jnp.float32)
+    total, picked = lax.fori_loop(0, vocab // step_rows, sum_step, (zeros, zeros))
+    own_sums[...] = jnp.concatenate(
+        [
+            jnp.broadcast_to(jnp.sum(total, axis=0, keepdims=True), (4, share)),
+            jnp.broadcast_to(jnp.sum(picked, axis=0, keepdims=True), (4, share)),
+        ],
+        axis=0,
+    )
+
+    def sum_copy(source, other):
+        return remote(own_sums, sums.at[source], send_sum.at[other], recv_sum.at[source], other)
 
     for other in others:
-        copy(me, other).start()
-    held[me] = x_ref[...]
+        sum_copy(me, other).start()
+    sums[me] = own_sums[...]
     for other in others:
-        copy(other, other).wait_recv()
-    out_ref[...] = jnp.sum(held[...], axis=0)
+        sum_copy(other, other).wait_recv()
+    both = jnp.sum(sums[...], axis=0)
+    denominator, picked = both[:1, :], both[4:5, :]
+    losses = jnp.sum(jnp.log(denominator) - picked, axis=1, keepdims=True)
+    loss_ref[...] = jnp.broadcast_to(losses, loss_ref.shape)
+
+    def slope_of(start, size):
+        value = logits[pl.ds(pl.multiple_of(start, 8), size), :]
+        entries = lax.broadcasted_iota(jnp.int32, value.shape, 0) + (me * vocab + start)
+        hit = (entries == labels).astype(jnp.float32)
+        return ((value / denominator - hit) / all_rows).T.astype(slopes.dtype)
+
+    def slope_step(number, carry):
+        start = pl.multiple_of(number * 128, 128)
+        slopes[:, pl.ds(start, 128)] = slope_of(start, 128)
+        return carry
+
+    lax.fori_loop(0, vocab // 128, slope_step, 0)
+    if vocab % 128:
+        start = vocab // 128 * 128
+        slopes[:, start:] = slope_of(start, vocab - start)
+
+    depth = share // per // pack
+
+    def packed(value):
+        rows = []
+        for index in range(per):
+            base = index * pack * depth
+            rows.append(
+                jnp.concatenate(
+                    [value[base + part * depth : base + (part + 1) * depth] for part in range(pack)], axis=1
+                )
+            )
+        return jnp.concatenate(rows, axis=0) if per > 1 else rows[0]
+
+    def near_copy(there):
+        return remote(near_out.at[there], near.at[there], send_near.at[there], recv_near.at[there], mate)
+
+    def far_copy(source, there):
+        return remote(far_out.at[there], far.at[source], send_far.at[there], recv_far.at[source], there * 2 + core)
+
+    def split(there):
+        if joined == 2:
+            lanes = pl.ds(pl.multiple_of(there * span, 128), span)
+            value = jnp.dot(slopes[...], weight[:, lanes], preferred_element_type=jnp.float32)
+            left, right = value[:, :features], value[:, features:]
+        else:
+            value = jnp.dot(slopes[...], weight[...], preferred_element_type=jnp.float32)
+            left = jnp.zeros((share, features), jnp.float32)
+            right = left
+            for index in range(chips):
+                base = index * 2 * features
+                left = jnp.where(there == index, value[:, base : base + features], left)
+                right = jnp.where(there == index, value[:, base + features : base + 2 * features], right)
+        first = core == 0
+        return jnp.where(first, left, right), jnp.where(first, right, left)
+
+    def target_of(index):
+        return lax.rem(chip + 1 + index, chips)
+
+    def pair_sum(index):
+        there = target_of(index)
+        near_copy(there).wait_recv()
+        return mine[lax.rem(index, 2)] + near[there].astype(jnp.float32)
+
+    def scatter_step(index, carry):
+        there = target_of(index)
+        kept, given = split(there)
+        mine[lax.rem(index, 2)] = packed(kept)
+        near_out[there] = packed(given).astype(near_out.dtype)
+        near_copy(there).start()
+
+        @pl.when(index > 0)
+        def _():
+            before = target_of(index - 1)
+            far_out[before] = pair_sum(index - 1).astype(far_out.dtype)
+            far_copy(chip, before).start()
+
+        return carry
+
+    lax.fori_loop(0, chips, scatter_step, 0)
+    result = pair_sum(chips - 1)
+    chips_out = [lax.rem(chip + step, chips) for step in range(1, chips)]
+    for there in chips_out:
+        far_copy(there, there).wait_recv()
+        result = result + far[there].astype(jnp.float32)
+    part_ref[...] = result.astype(part_ref.dtype)
+
+    @pl.when(is_end)
+    def _():
+        for index in range(1, chips):
+            line_copy(chip, jnp.where(chip == 0, index, chips - 1 - index)).wait_send()
+
+    if chips > 2:
+        @pl.when(jnp.logical_not(is_end))
+        def _():
+            line_copy(chip, chip + 1).wait_send()
+            line_copy(chip, chip - 1).wait_send()
+
+    mate_copy(chip, core).wait_send()
+    for index in range(1, chips):
+        origin = origin_of(chips, chip, index)
+        onward, wanted = onward_of(chips, chip, origin)
+
+        @pl.when(wanted)
+        def _():
+            line_copy(origin, jnp.clip(onward, 0, chips - 1)).wait_send()
+
+        mate_copy(origin, core).wait_send()
     for other in others:
-        copy(me, other).wait_send()
-
-
-def exchange(x, collective_id):
-    tensors = lax.axis_size("tensor")
+        sum_copy(me, other).wait_send()
+    for there in chips_out + [chip]:
+        near_copy(there).wait_send()
+    for there in chips_out:
+        far_copy(chip, there).wait_send()
+
+
+def head(hidden, labels, head_weight, pack, per):
+    sections, tensors = lax.axis_size("section"), lax.axis_size("tensor")
+    chips = tensors // 2
+    features, tokens = hidden.shape
+    vocab, width = head_weight.shape
+    share = tokens // sections
+    groups = chips if (2 * features) % 128 == 0 else 1
+    dma = pltpu.SemaphoreType.DMA
     vmem = pl.BlockSpec(memory_space=pltpu.VMEM)
-    dma = pltpu.SemaphoreType.DMA
+    hbm = pl.BlockSpec(memory_space=pl.ANY)
+    dense = (share // pack, pack * features)
+    held = pltpu.VMEM((chips,) + dense, jnp.bfloat16)
     return pl.pallas_call(
-        functools.partial(exchange_kernel, tensors),
-        out_shape=jax.ShapeDtypeStruct(x.shape, x.dtype),
-        in_specs=[vmem],
-        out_specs=vmem,
-        scratch_shapes=[pltpu.VMEM((tensors,) + x.shape, x.dtype), dma((tensors,)), dma((tensors,))],
+        functools.partial(head_kernel, tensors, pack, per),
+        out_shape=(
+            jax.ShapeDtypeStruct(dense, jnp.bfloat16),
+            jax.ShapeDtypeStruct((8, 128), jnp.float32),
+        ),
+        in_specs=[hbm, vmem, hbm],
+        out_specs=(vmem, vmem),
+        scratch_shapes=[
+            pltpu.VMEM((vocab, width), jnp.bfloat16),
+            pltpu.VMEM((width, share), jnp.bfloat16),
+            pltpu.VMEM((vocab, share), jnp.float32),
+            pltpu.VMEM((share, vocab), jnp.bfloat16),
+            pltpu.VMEM((2,) + dense, jnp.float32),
+            held, held, held, held,
+            pltpu.VMEM((8, share), jnp.float32),
+            pltpu.VMEM((tensors, 8, share), jnp.float32),
+            dma((groups,)),
+            dma((2 * chips,)),
+            dma((chips,)),
+            dma((chips,)),
+            dma((chips,)),
+            dma((tensors,)),
+            dma((tensors,)),
+            dma((chips,)),
+            dma((chips,)),
+            dma((chips,)),
+            dma((chips,)),
+            dma((1,)),
+        ],
         compiler_params=pltpu.CompilerParams(
-            collective_id=collective_id, has_side_effects=True, vmem_limit_bytes=24 * 1024 * 1024
+            collective_id=1, has_side_effects=True, vmem_limit_bytes=67_000_000
         ),
-    )(x)
-
-
-def packed_sum(parts, collective_id):
-    flat = jnp.concatenate([jnp.reshape(part, (-1,)) for part in parts])
-    rows = -(-flat.shape[0] // 1024) * 8
-    flat = jnp.pad(flat, (0, rows * 128 - flat.shape[0])).reshape(rows, 128)
-    flat = exchange(flat, collective_id).reshape(-1)
-    sums, start = [], 0
-    for part in parts:
-        sums.append(flat[start : start + part.size].reshape(part.shape))
-        start += part.size
-    return sums
+    )(hidden, labels, head_weight)
 
 
 def step_kernel(
@@ -299,16 +411,6 @@
             loss_ref, loss_buf.at[source], send_loss.at[there], recv_loss.at[source], {"section": there}
         )
 
-    def origin_of(index):
-        if index == 0:
-            return chip
-        near_side = jnp.where(chip * 2 < chips, -1, 1)
-        both = jnp.minimum(chip, chips - 1 - chip)
-        paired = index <= 2 * both
-        distance = jnp.where(paired, (index + 1) // 2, index - both)
-        toward_near = paired & (index % 2 == 0)
-        return chip + jnp.where(toward_near, near_side, -near_side) * distance
-
     barrier = pltpu.get_barrier_semaphore()
     greeted = [{"tensor": mate}]
     greeted += [{"tensor": rem(chip + step, chips) * 2 + core} for step in range(1, chips)]
@@ -345,7 +447,7 @@
         @pl.when(is_end)
         def _():
             for index in range(1, chips):
-                line_copy(step, chip, jnp.where(chip == 0, chips - index, index - 1)).start()
+                line_copy(step, chip, jnp.where(chip == 0, index, chips - 1 - index)).start()
 
         if chips > 2:
             @pl.when(jnp.logical_not(is_end))
@@ -354,11 +456,6 @@
                 line_copy(step, chip, chip - 1).start()
 
         mate_copy(step, chip, core).start()
-
-    def forwards(origin):
-        onward = jnp.where(origin < chip, chip + 1, chip - 1)
-        inner = (origin > 0) & (origin < chips - 1)
-        return onward, inner & (onward >= 0) & (onward < chips)
 
     def assemble(step, first):
         for part in range(pack):
@@ -379,7 +476,7 @@
         acc_ref[...] = value if fresh else acc_ref[...] + value
 
     def finish(step, index):
-        origin = origin_of(index)
+        origin = origin_of(chips, chip, index)
         mate_copy(step, origin, 1 - core).wait_recv()
         if joined == 2:
             assemble(step, origin * 2)
@@ -419,9 +516,9 @@
                 def _():
                     launch(jnp.minimum(step + 1, count - 1))
 
-            origin = origin_of(index)
+            origin = origin_of(chips, chip, index)
             line_copy(step, origin, chip).wait_recv()
-            onward, wanted = forwards(origin)
+            onward, wanted = onward_of(chips, chip, origin)
 
             @pl.when(wanted)
             def _():
@@ -566,7 +663,7 @@
         @pl.when(is_end)
         def _():
             for index in range(1, chips):
-                line_copy(step, chip, jnp.where(chip == 0, chips - index, index - 1)).wait_send()
+                line_copy(step, chip, jnp.where(chip == 0, index, chips - 1 - index)).wait_send()
 
         if chips > 2:
             @pl.when(jnp.logical_not(is_end))
@@ -576,8 +673,8 @@
 
         mate_copy(step, chip, core).wait_send()
         for index in range(1, chips):
-            origin = origin_of(index)
-            onward, wanted = forwards(origin)
+            origin = origin_of(chips, chip, index)
+            onward, wanted = onward_of(chips, chip, origin)
 
             @pl.when(wanted)
             def _():
@@ -601,48 +698,72 @@
     mate_total(core).wait_send()
 
 
-def update_kernel(weight_ref, grad_ref, row_ref, col_ref, out_ref):
-    rows, width = out_ref.shape
+def update_kernel(
+    pack, size, weight_ref, grad_ref, scale_ref, col_ref, carried_ref, row_ref, col_in, total_ref,
+    weight_out, carried_out, row_out, col_out, loss_out,
+):
+    rows, width = weight_out.shape
     group = 512 if width % 512 == 0 else 128
+
+    @pl.when(pl.program_id(0) == 0)
+    def _():
+        features, tokens = carried_out.shape
+        depth = size // pack
+        for start in range(0, tokens, 2 * size):
+            pieces = []
+            for share in (start // size, start // size + 1):
+                entries = carried_ref[share * depth : (share + 1) * depth, :].astype(jnp.float32)
+                pieces += [entries[:, part * features : (part + 1) * features] for part in range(pack)]
+            joined = jnp.concatenate(pieces, axis=0)
+            carried_out[:, start : start + 2 * size] = joined.T.astype(carried_out.dtype)
+        row_out[...] = jnp.broadcast_to(row_ref[...], (features, 128)).T[:1, :]
+        col_out[...] = col_in[...]
+        loss_out[...] = total_ref[:1, :1] / tokens
+
     for start in range(0, rows, 16):
-        scale = jnp.broadcast_to(row_ref[start : start + 16, :], (16, group))
+        scale = jnp.broadcast_to(scale_ref[start : start + 16, :], (16, group))
         for lane in range(0, width, group):
             change = grad_ref[start : start + 16, lane : lane + group].astype(jnp.float32)
             change = change * (scale * col_ref[:, lane : lane + group])
             entries = weight_ref[start : start + 16, lane : lane + group].astype(jnp.float32)
-            out_ref[start : start + 16, lane : lane + group] = (entries - change).astype(out_ref.dtype)
-
-
-def update(weight, grad, row_scale, col_scale):
+            weight_out[start : start + 16, lane : lane + group] = (entries - change).astype(weight_out.dtype)
+
+
+def update(pack, size, tokens, weight, grad, row_scale, col_scale, outputs, row_new, col_new, total):
     features, width = weight.shape
     rows = max(size for size in range(16, 65, 16) if features % size == 0)
     tile = pl.BlockSpec((rows, width), lambda index: (index, 0))
+
+    def whole(shape):
+        return pl.BlockSpec(shape, lambda index: (0, 0))
+
     return pl.pallas_call(
-        update_kernel,
+        functools.partial(update_kernel, pack, size),
         grid=(features // rows,),
-        out_shape=jax.ShapeDtypeStruct((features, width), jnp.bfloat16),
+        out_shape=(
+            jax.ShapeDtypeStruct((features, width), jnp.bfloat16),
+            jax.ShapeDtypeStruct((features, tokens), jnp.bfloat16),
+            jax.ShapeDtypeStruct((1, features), jnp.float32),
+            jax.ShapeDtypeStruct((1, width), jnp.float32),
+            jax.ShapeDtypeStruct((1, 1), jnp.float32),
+        ),
         in_specs=[
-            tile, tile,
-            pl.BlockSpec((rows, 1), lambda index: (index, 0)),
-            pl.BlockSpec((1, width), lambda index: (0, 0)),
+            tile, tile, pl.BlockSpec((rows, 1), lambda index: (index, 0)), whole((1, width)),
+            whole(outputs.shape), whole((features, 1)), whole((1, width)), whole((8, 128)),
         ],
-        out_specs=tile,
-        compiler_params=pltpu.CompilerParams(vmem_limit_bytes=16 * 1024 * 1024),
-    )(weight, grad, row_scale, col_scale)
-
-
-def step(part, part_loss, saved, local_weight, row_state, col_state):
+        out_specs=(tile, whole((features, tokens)), whole((1, features)), whole((1, width)), whole((1, 1))),
+        compiler_params=pltpu.CompilerParams(vmem_limit_bytes=56 * 1024 * 1024),
+    )(weight, grad, row_scale, col_scale, outputs, row_new, col_new, total)
+
+
+def step(part, losses, saved, local_weight, row_state, col_state, pack, count):
     sections, tensors = lax.axis_size("section"), lax.axis_size("tensor")
     features, tokens = saved.shape
     width = features * tensors
     chips = tensors // 2
-    count = 2 * sections
     size = tokens // count
-    pack = 2 if (2 * features) % 128 == 0 and (size // 2) % 16 == 0 else 1
     group = 512 if width % 512 == 0 else 128
     lines = -(-(width // group + 2) // 8) * 8
-    part = part.reshape(count // sections, pack, size // pack, features)
-    part = jnp.transpose(part, (0, 2, 1, 3)).reshape(tokens // sections // pack, pack * features)
     dma = pltpu.SemaphoreType.DMA
     vmem = pl.BlockSpec(memory_space=pltpu.VMEM)
     hbm = pl.BlockSpec(memory_space=pl.ANY)
@@ -694,59 +815,21 @@
         compiler_params=pltpu.CompilerParams(
             collective_id=0, has_side_effects=True, vmem_limit_bytes=57 * 1024 * 1024
         ),
-    )(part, jnp.full((8, 128), part_loss, jnp.float32), saved, row_state, col_state, local_weight)
-    outputs = outputs.reshape(count, size // pack, pack, features)
-    outputs = jnp.transpose(outputs, (0, 2, 1, 3)).reshape(tokens, features)
-    weight = update(local_weight, grad, row_scale, col_scale)
-    return outputs, weight, total, row_new, col_new
+    )(part, losses, saved, row_state, col_state, local_weight)
+    return update(pack, size, tokens, local_weight, grad, row_scale, col_scale, outputs, row_new, col_new, total)
 
 
 def body(hidden_last, labels, head_weight, layer_inputs, weights, row_state, col_state):
-    section_count = lax.axis_size("section")
-    section_index = lax.axis_index("section")
-    all_rows = labels.shape[0]
-    vocab_local = head_weight.shape[1]
-    local_weight = weights[0]
-    saved_all = layer_inputs[0]
-    columns = lax.axis_index("tensor") * vocab_local + lax.iota(jnp.int32, vocab_local)
-    share_rows = all_rows // section_count
-    row_start = section_index * share_rows
-    hidden_rows = lax.dynamic_slice_in_dim(hidden_last, row_start, share_rows, 0)
-    head_slice = head_weight
-    logits = lax.dot_general(
-        gather_rows(hidden_rows.T, 3),
-        head_slice,
-        (((0,), (0,)), ((), ())),
-        preferred_element_type=jnp.float32,
+    sections, tensors = lax.axis_size("section"), lax.axis_size("tensor")
+    tokens, features = hidden_last.shape
+    count = 2 * sections
+    size = tokens // count
+    pack = 2 if (2 * features) % 128 == 0 and (size // 2) % 16 == 0 else 1
+    part, losses = head(hidden_last.T, labels.reshape(1, -1), head_weight.T, pack, count // sections)
+    new_weight, outputs, row_new, col_new, loss = step(
+        part, losses, layer_inputs[0].T, weights[0], row_state.reshape(-1, 1), col_state, pack, count
     )
-    exponent = jnp.exp(logits)
-    label_hit = (
-        lax.dynamic_slice_in_dim(labels, row_start, share_rows, 0)[:, None] == columns[None, :]
-    )
-    denominator, picked = packed_sum(
-        (
-            jnp.sum(exponent, axis=1),
-            jnp.sum(jnp.where(label_hit, logits, jnp.zeros_like(logits)), axis=1),
-        ),
-        1,
-    )
-    losses = jnp.log(denominator) - picked
-    logit_grad = (
-        (exponent / denominator[:, None] - label_hit.astype(jnp.float32)) / all_rows
-    ).astype(jnp.bfloat16)
-    head_slice = head_weight
-    part_grad = scatter_rows(
-        lax.dot_general(
-            head_slice, logit_grad, (((1,), (1,)), ((), ())), preferred_element_type=jnp.float32
-        ).astype(jnp.bfloat16),
-        4,
-    )
-    part_loss = jnp.sum(losses)
-    outputs, new_weight, total, row_new, col_new = step(
-        part_grad.T, part_loss, saved_all.T, local_weight, row_state.reshape(-1, 1), col_state
-    )
-    loss = total[0, 0] / all_rows
-    return (loss, outputs[None], new_weight[None], row_new.reshape(1, -1), col_new)
+    return (loss[0, 0], outputs.T[None], new_weight[None], row_new, col_new)
 
 
 def solution(mesh):

time: 298 us -> 251 us (0.84)
  matrix products: 50.4 us -> 0 us
  Pallas kernels: 223 us -> 249 us
  local copies, waits for them, and re-layouts: 20 us -> 0.96 us
    dot_general x2 -> x0, matrix products: 50.4 us -> none  [the longest x1 28.3 us: body(): lax.dot_general(head_slice, logit_grad, (((1,), (1,)), ((), ())), preferr...]
    pallas_call x4 -> x2, Pallas kernels: 55.8 us -> 94.5 us  [the longest x1 75.8 us: head(): pl.pallas_call(functools.partial(head_kernel, tensors, pack, per), out_sh...]
    pallas_call x1, Pallas kernels: 167 us -> 154 us  [step(): pl.pallas_call(functools.partial(step_kernel, sections, tensors, count, p...]
    unnamed x16 -> x2, local copies, waits for them, and re-layouts: 10.5 us -> 0.01 us
    reshape x4 -> x0, local copies, waits for them, and re-layouts: 4.21 us -> none  [the longest x2 2.75 us: step(): outputs = outputs.reshape(count, size // pack, pack, features)]
where the time goes in v3:
time: 251 us; the launch traced here: 250 us
  Pallas kernels  249 us (99%)
    pallas_call x1, Pallas kernels, step(): pl.pallas_call(functools.partial(step_kernel, sections, tensors, count, p...  154 us
    pallas_call x1, Pallas kernels, head(): pl.pallas_call(functools.partial(head_kernel, tensors, pack, per), out_sh...  75.8 us
    pallas_call x1, Pallas kernels, update(): pl.pallas_call(functools.partial(update_kernel, pack, size), grid=(featur...  18.8 us

profile of v3, /device:TPU:1, one launch (start us, length us, event | category | flops | bytes accessed | tf_op | source)
XLA Modules:
  0.0 250.3 jit_solution(9287541312156988970)
XLA Ops:
  0.6 0.0 copy-start
  0.6 75.8 %shard_map.110 = (bf16[64,1664]{1,0:T(8,128)(2,1)}, f32[8,128]{1,0:T(8,128)}) custom-call(bf16[832,512]{1,0:T(8,128)(2,1)} %bitcast.17, s32[1,512]{1,0:T(1,128)} %bitcast.19, bf16[4000,6656]{1,0:T(8,128)(2,1)} %bitcast.13), custom_call_target="tpu_custom_call" | custom-call | tf_op jit(solution)/shard_map/pallas_call | solution.py:300
  76.4 0.0 copy-done
  76.4 1.0 copy.12.row_ref
  77.4 154.1 %shard_map.111 = (bf16[256,1664]{1,0:T(8,128)(2,1)}, bf16[832,6656]{1,0:T(8,128)(2,1)}, f32[8,128]{1,0:T(8,128)}, f32[832,1]{1,0:T(8,128)}, f32[832,1]{1,0:T(8,1...) custom-call(bf16[64,1664]{1,0:T(8,128)(2,1)} %get-tuple-element.19.part_ref, f32[8,128]{1,0:T(8,128)} %get-tuple-element.20.loss_ref, ...), custom_call_target="tpu_custom_call" | custom-call | tf_op jit(solution)/shard_map/pallas_call | solution.py:771
  231.5 18.8 %shard_map.112 = (bf16[832,6656]{1,0:T(8,128)(2,1)}, bf16[832,512]{1,0:T(8,128)(2,1)}, f32[1,832]{1,0:T(1,128)}, f32[1,6656]{1,0:T(1,128)}, f32[1,1]{1,0:T(1,128)}) custom-call(bf16[832,6656]{1,0:T(8,128)(2,1)} %bitcast.15, bf16[832,6656]{1,0:T(8,128)(2,1)} %get-tuple-element.21.grad_ref, f32[832,1]{1,0:T(8,128)} %get-tuple-element.22.scale_ref, ...), custom_call_target="tpu_custom_call" | custom-call | tf_op jit(solution)/shard_map/pallas_call | solution.py:740
Async XLA Ops:
  0.6 75.8 %copy-start = (f32[1,832]{1,0:T(1,128)S(1)}, f32[1,832]{1,0:T(1,128)}, u32[]{:S(2)}) copy-start(f32[1,832]{1,0:T(1,128)} %param.12) | copy-start | bytes 9988

commit v4 on v3

--- a/solution.py
+++ b/solution.py
@@ -80,9 +80,6 @@
         return pltpu.make_async_copy(hidden_ref.at[:, my_tokens], block(me), local_sem.at[0])
 
     own_copy().start()
-    for index in range(groups):
-        weight_copy(index).start()
-
     barrier = pltpu.get_barrier_semaphore()
     others = [lax.rem(me + step, tensors) for step in range(1, tensors)]
     for other in others:
@@ -103,6 +100,8 @@
             line_copy(chip, chip - 1).start()
 
     mate_copy(chip, core).start()
+    for index in range(min(groups, 2)):
+        weight_copy(index).start()
 
     tile = max([size for size in range(16, 801, 16) if vocab % size == 0], default=vocab)
 
@@ -118,24 +117,35 @@
 
         lax.fori_loop(0, vocab // tile, rows_step, 0)
 
-    for index in range(chips):
+    def arrive(index):
         origin = origin_of(chips, chip, index)
-        if index:
-            line_copy(origin, chip).wait_recv()
-            onward, wanted = onward_of(chips, chip, origin)
-
-            @pl.when(wanted)
-            def _():
-                line_copy(origin, jnp.clip(onward, 0, chips - 1)).start()
-
-            mate_copy(origin, core).start()
-        mate_copy(origin, 1 - core).wait_recv()
+        line_copy(origin, chip).wait_recv()
+        onward, wanted = onward_of(chips, chip, origin)
+
+        @pl.when(wanted)
+        def _():
+            line_copy(origin, jnp.clip(onward, 0, chips - 1)).start()
+
+        mate_copy(origin, core).start()
+        if index + 1 < groups:
+            weight_copy(index + 1).start()
+
+    def consume(index):
+        mate_copy(origin_of(chips, chip, index), 1 - core).wait_recv()
         if joined == 2:
             weight_copy(index).wait()
             product(index, index == 0)
         elif index == chips - 1:
             weight_copy(0).wait()
             product(0, True)
+
+    for index in range(1, chips):
+        arrive(index)
+        if index == 1:
+            consume(0)
+        consume(index)
+    if chips == 1:
+        consume(0)
 
     labels = labels_ref[:, my_tokens]
     step_rows = max(size for size in range(8, 201, 8) if vocab % size == 0)
@@ -178,7 +188,7 @@
         value = logits[pl.ds(pl.multiple_of(start, 8), size), :]
         entries = lax.broadcasted_iota(jnp.int32, value.shape, 0) + (me * vocab + start)
         hit = (entries == labels).astype(jnp.float32)
-        return ((value / denominator - hit) / all_rows).T.astype(slopes.dtype)
+        return ((value / denominator - hit) / all_rows).astype(slopes.dtype).T
 
     def slope_step(number, carry):
         start = pl.multiple_of(number * 128, 128)
@@ -336,7 +346,7 @@
 def step_kernel(
     sections, tensors, count, pack, part_ref, loss_ref, x_ref, row_ref, col_ref, w_ref,
     out_ref, grad_out, total_ref, row_out, row_scale, col_out, col_scale,
-    weight_ref, stage, held, carried, grad, acc_ref, row_acc, row_full, loss_buf, vectors, near, pair_sum, spread, final,
+    flipped, stage, held, carried, grad, acc_ref, row_acc, row_full, loss_buf, vectors, near, pair_sum, spread, final,
     send_x, recv_x, send_z, recv_z, send_mate, recv_mate, send_loss, recv_loss, local_sem, head_sem,
     send_sum, recv_sum, send_far, recv_far, stage_sem,
 ):
@@ -403,8 +413,10 @@
             part_ref.at[pl.ds(index * depth, depth), :], block(me, index), local_sem.at[index]
         )
 
-    def weight_copy():
-        return pltpu.make_async_copy(w_ref, weight_ref, local_sem.at[per])
+    def weight_copy(index):
+        lanes = pl.ds(pl.multiple_of(index * span, 128), span)
+        slot = rem(index, 2)
+        return pltpu.make_async_copy(w_ref.at[:, lanes], stage.at[slot], local_sem.at[per + slot])
 
     def loss_copy(source, there):
         return remote(
@@ -415,7 +427,7 @@
     greeted = [{"tensor": mate}]
     greeted += [{"tensor": rem(chip + step, chips) * 2 + core} for step in range(1, chips)]
     greeted += [{"section": rem(section + step, sections)} for step in range(1, sections)]
-    weight_copy().start()
+    groups = tensors // joined
     for device in greeted:
         pl.semaphore_signal(barrier, inc=1, device_id=device, device_id_type=MESH)
     pl.semaphore_wait(barrier, len(greeted))
@@ -434,6 +446,7 @@
         loss_copy(section, rem(section + step, sections)).start()
 
     is_end = (chip == 0) | (chip == chips - 1)
+    ahead = 2
 
     def launch(step):
         @pl.when((section == last) & (step < per))
@@ -469,10 +482,7 @@
 
     def product(step, first, fresh):
         lanes = pl.ds(pl.multiple_of(first * features, 128), span)
-        value = lax.dot_general(
-            carried[rows_of(step), lanes], weight_ref[:, lanes], (((1,), (1,)), ((), ())),
-            preferred_element_type=jnp.float32,
-        )
+        value = jnp.dot(carried[rows_of(step), lanes], flipped[lanes, :], preferred_element_type=jnp.float32)
         acc_ref[...] = value if fresh else acc_ref[...] + value
 
     def finish(step, index):
@@ -485,36 +495,50 @@
             assemble(step, 0)
             product(step, 0, True)
 
-    launch(0)
-    weight_copy().wait()
-
-    def add_squares():
-        def rows_step(index, inner):
-            entries = weight_ref[pl.ds(pl.multiple_of(index * 16, 16), 16), :].astype(jnp.float32)
-            return inner + jnp.sum(jnp.reshape(entries * entries, (2, 8, width)), axis=0)
-
-        sums = lax.fori_loop(0, features // 16, rows_step, jnp.zeros((8, width), jnp.float32))
-        folded = sums[:, :128]
-        for start in range(128, width, 128):
-            folded = folded + sums[:, start : start + 128]
-        vectors[1, pl.ds(used + 1, 1), :] = jnp.broadcast_to(jnp.sum(folded, keepdims=True), (1, group))
-
+    @pl.when(section == last)
+    def _():
+        for index in range(ahead):
+            launch(index)
+
+    for index in range(min(groups, 2)):
+        weight_copy(index).start()
     vectors[...] = jnp.zeros_like(vectors)
+
+    def flip(index, inner):
+        slot = rem(index, 2)
+        weight_copy(index).wait()
+        lanes = pl.ds(pl.multiple_of(index * span, 128), span)
+        flipped[lanes, :] = stage[slot].T
+        for start in range(0, features, 16):
+            entries = stage[slot, start : start + 16, :].astype(jnp.float32)
+            inner = inner + jnp.sum(jnp.reshape(entries * entries, (2, 8, span)), axis=0)
+
+        @pl.when(index + 2 < groups)
+        def _():
+            weight_copy(index + 2).start()
+
+        return inner
+
+    squares = lax.fori_loop(0, groups, flip, jnp.zeros((8, span), jnp.float32))
+    vectors[1, pl.ds(used + 1, 1), :] = jnp.broadcast_to(jnp.sum(squares, keepdims=True), (1, group))
 
     @pl.when(section != last)
     def _():
-        add_squares()
+        for index in range(ahead):
+            launch(index)
 
     half = count // 2
     low = tokens // 2
-    cut = width // half
+    pieces = 4 if half % 4 == 0 and width % 512 == 0 else 1
+    stride = half // pieces
+    cut = width // pieces
 
     def advance(step, carry):
         for index in range(1, chips):
             if index == min(2, chips - 1):
-                @pl.when(step + 1 < count)
+                @pl.when(step + ahead < count)
                 def _():
-                    launch(jnp.minimum(step + 1, count - 1))
+                    launch(jnp.minimum(step + ahead, count - 1))
 
             origin = origin_of(chips, chip, index)
             line_copy(step, origin, chip).wait_recv()
@@ -535,9 +559,9 @@
         def _():
             down_copy(step).start()
 
-        @pl.when(step >= half)
-        def _():
-            lanes = pl.ds(pl.multiple_of((step - half) * cut, 128), cut)
+        @pl.when((step >= half) & (rem(step, stride) == 0))
+        def _():
+            lanes = pl.ds(pl.multiple_of((step - half) // stride * cut, 128), cut)
             grad[:, lanes] = jnp.dot(
                 x_ref[:, low:], carried[low:, lanes], preferred_element_type=jnp.float32
             )
@@ -546,16 +570,12 @@
 
     lax.fori_loop(0, count, advance, 0)
 
-    @pl.when(section == last)
-    def _():
-        add_squares()
-
     row_acc[...] = jnp.zeros_like(row_acc)
 
     def stage_copy(index):
         lanes = pl.ds(pl.multiple_of(index * group, 128), group)
         slot = rem(index, 2)
-        return pltpu.make_async_copy(stage.at[slot], grad_out.at[:, lanes], stage_sem.at[slot])
+        return pltpu.make_async_copy(stage.at[slot, :, pl.ds(0, group)], grad_out.at[:, lanes], stage_sem.at[slot])
 
     def gather_squares(index, carry):
         lanes = pl.ds(pl.multiple_of(index * group, 128), group)
@@ -572,7 +592,7 @@
         inner = jnp.zeros((8, group), jnp.float32)
         for start in range(0, features, 16):
             entries = grad[start : start + 16, lanes]
-            stage[slot, start : start + 16, :] = entries.astype(stage.dtype)
+            stage[slot, start : start + 16, :group] = entries.astype(stage.dtype)
             squares = entries * entries + tiny_term
             folded = squares[:, :128]
             for lane in range(128, group, 128):
@@ -699,47 +719,77 @@
 
 
 def update_kernel(
-    pack, size, weight_ref, grad_ref, scale_ref, col_ref, carried_ref, row_ref, col_in, total_ref,
-    weight_out, carried_out, row_out, col_out, loss_out,
+    pack, size, scale_ref, col_ref, carried_ref, row_ref, col_in, total_ref, weight_ref, grad_ref,
+    weight_out, carried_out, row_out, col_out, loss_out, entries_buf, grad_buf, weight_sem, grad_sem, out_sem,
 ):
-    rows, width = weight_out.shape
+    count, rows, width = entries_buf.shape
     group = 512 if width % 512 == 0 else 128
-
-    @pl.when(pl.program_id(0) == 0)
-    def _():
-        features, tokens = carried_out.shape
-        depth = size // pack
-        for start in range(0, tokens, 2 * size):
-            pieces = []
-            for share in (start // size, start // size + 1):
-                entries = carried_ref[share * depth : (share + 1) * depth, :].astype(jnp.float32)
-                pieces += [entries[:, part * features : (part + 1) * features] for part in range(pack)]
-            joined = jnp.concatenate(pieces, axis=0)
-            carried_out[:, start : start + 2 * size] = joined.T.astype(carried_out.dtype)
-        row_out[...] = jnp.broadcast_to(row_ref[...], (features, 128)).T[:1, :]
-        col_out[...] = col_in[...]
-        loss_out[...] = total_ref[:1, :1] / tokens
-
-    for start in range(0, rows, 16):
-        scale = jnp.broadcast_to(scale_ref[start : start + 16, :], (16, group))
-        for lane in range(0, width, group):
-            change = grad_ref[start : start + 16, lane : lane + group].astype(jnp.float32)
-            change = change * (scale * col_ref[:, lane : lane + group])
-            entries = weight_ref[start : start + 16, lane : lane + group].astype(jnp.float32)
-            weight_out[start : start + 16, lane : lane + group] = (entries - change).astype(weight_out.dtype)
+    features, tokens = carried_out.shape
+
+    def rows_of(index):
+        return pl.ds(pl.multiple_of(index * rows, 16), rows)
+
+    def weight_copy(index):
+        return pltpu.make_async_copy(weight_ref.at[rows_of(index), :], entries_buf.at[index], weight_sem.at[index])
+
+    def grad_copy(index):
+        return pltpu.make_async_copy(grad_ref.at[rows_of(index), :], grad_buf.at[index], grad_sem.at[index])
+
+    def out_copy(index):
+        return pltpu.make_async_copy(entries_buf.at[index], weight_out.at[rows_of(index), :], out_sem.at[index])
+
+    def fetch(index, carry):
+        weight_copy(index).start()
+        grad_copy(index).start()
+        return carry
+
+    lax.fori_loop(0, count, fetch, 0)
+    depth = size // pack
+    for start in range(0, tokens, 128):
+        pieces = []
+        for share in range(start // size, (start + 128) // size):
+            entries = carried_ref[share * depth : (share + 1) * depth, :].astype(jnp.float32)
+            pieces += [entries[:, part * features : (part + 1) * features] for part in range(pack)]
+        joined = jnp.concatenate(pieces, axis=0)
+        carried_out[:, start : start + 128] = joined.T.astype(carried_out.dtype)
+    row_out[...] = jnp.broadcast_to(row_ref[...], (features, 128)).T[:1, :]
+    col_out[...] = col_in[...]
+    loss_out[...] = total_ref[:1, :1] / tokens
+
+    def change(index, carry):
+        weight_copy(index).wait()
+        grad_copy(index).wait()
+        scales = scale_ref[rows_of(index), :]
+        for start in range(0, rows, 16):
+            scale = jnp.broadcast_to(scales[start : start + 16, :], (16, group))
+            for lane in range(0, width, group):
+                lanes = slice(lane, lane + group)
+                moved = grad_buf[index, start : start + 16, lanes].astype(jnp.float32)
+                moved = moved * (scale * col_ref[:, lanes])
+                entries = entries_buf[index, start : start + 16, lanes].astype(jnp.float32)
+                entries_buf[index, start : start + 16, lanes] = (entries - moved).astype(entries_buf.dtype)
+        out_copy(index).start()
+        return carry
+
+    lax.fori_loop(0, count, change, 0)
+
+    def finish(index, carry):
+        out_copy(index).wait()
+        return carry
+
+    lax.fori_loop(0, count, finish, 0)
 
 
 def update(pack, size, tokens, weight, grad, row_scale, col_scale, outputs, row_new, col_new, total):
     features, width = weight.shape
     rows = max(size for size in range(16, 65, 16) if features % size == 0)
-    tile = pl.BlockSpec((rows, width), lambda index: (index, 0))
-
-    def whole(shape):
-        return pl.BlockSpec(shape, lambda index: (0, 0))
-
+    count = features // rows
+    vmem = pl.BlockSpec(memory_space=pltpu.VMEM)
+    hbm = pl.BlockSpec(memory_space=pl.ANY)
+    dma = pltpu.SemaphoreType.DMA((count,))
+    held = pltpu.VMEM((count, rows, width), jnp.bfloat16)
     return pl.pallas_call(
         functools.partial(update_kernel, pack, size),
-        grid=(features // rows,),
         out_shape=(
             jax.ShapeDtypeStruct((features, width), jnp.bfloat16),
             jax.ShapeDtypeStruct((features, tokens), jnp.bfloat16),
@@ -747,13 +797,11 @@
             jax.ShapeDtypeStruct((1, width), jnp.float32),
             jax.ShapeDtypeStruct((1, 1), jnp.float32),
         ),
-        in_specs=[
-            tile, tile, pl.BlockSpec((rows, 1), lambda index: (index, 0)), whole((1, width)),
-            whole(outputs.shape), whole((features, 1)), whole((1, width)), whole((8, 128)),
-        ],
-        out_specs=(tile, whole((features, tokens)), whole((1, features)), whole((1, width)), whole((1, 1))),
-        compiler_params=pltpu.CompilerParams(vmem_limit_bytes=56 * 1024 * 1024),
-    )(weight, grad, row_scale, col_scale, outputs, row_new, col_new, total)
+        in_specs=[vmem] * 6 + [hbm] * 2,
+        out_specs=(hbm,) + (vmem,) * 4,
+        scratch_shapes=[held, held, dma, dma, dma],
+        compiler_params=pltpu.CompilerParams(vmem_limit_bytes=60 * 1024 * 1024),
+    )(row_scale, col_scale, outputs, row_new, col_new, total, weight, grad)
 
 
 def step(part, losses, saved, local_weight, row_state, col_state, pack, count):
@@ -763,6 +811,7 @@
     chips = tensors // 2
     size = tokens // count
     group = 512 if width % 512 == 0 else 128
+    span = 2 * features if (2 * features) % 128 == 0 else width
     lines = -(-(width // group + 2) // 8) * 8
     dma = pltpu.SemaphoreType.DMA
     vmem = pl.BlockSpec(memory_space=pltpu.VMEM)
@@ -782,8 +831,8 @@
         in_specs=[vmem] * 5 + [hbm],
         out_specs=(vmem, hbm) + (vmem,) * 5,
         scratch_shapes=[
-            pltpu.VMEM((features, width), jnp.bfloat16),
-            pltpu.VMEM((2, features, group), jnp.bfloat16),
+            pltpu.VMEM((width, features), jnp.bfloat16),
+            pltpu.VMEM((2, features, span), jnp.bfloat16),
             pltpu.VMEM((tensors, tokens // pack, pack * features), jnp.bfloat16),
             pltpu.VMEM((tokens, width), jnp.bfloat16),
             pltpu.VMEM((features, width), jnp.float32),
@@ -804,7 +853,7 @@
             dma((count, chips)),
             dma((sections,)),
             dma((sections,)),
-            dma((count // sections + 1,)),
+            dma((count // sections + 2,)),
             dma((count // sections,)),
             dma((2,)),
             dma((2,)),
@@ -813,7 +862,7 @@
             dma((2,)),
         ],
         compiler_params=pltpu.CompilerParams(
-            collective_id=0, has_side_effects=True, vmem_limit_bytes=57 * 1024 * 1024
+            collective_id=0, has_side_effects=True, vmem_limit_bytes=66_000_000
         ),
     )(part, losses, saved, row_state, col_state, local_weight)
     return update(pack, size, tokens, local_weight, grad, row_scale, col_scale, outputs, row_new, col_new, total)
@@ -822,7 +871,7 @@
 def body(hidden_last, labels, head_weight, layer_inputs, weights, row_state, col_state):
     sections, tensors = lax.axis_size("section"), lax.axis_size("tensor")
     tokens, features = hidden_last.shape
-    count = 2 * sections
+    count = 4 * sections
     size = tokens // count
     pack = 2 if (2 * features) % 128 == 0 and (size // 2) % 16 == 0 else 1
     part, losses = head(hidden_last.T, labels.reshape(1, -1), head_weight.T, pack, count // sections)

time: 251 us -> 223 us (0.89)
  Pallas kernels: 249 us -> 221 us
    pallas_call x1, Pallas kernels: 75.8 us -> 62.4 us  [head(): pl.pallas_call(functools.partial(head_kernel, tensors, pack, per), out_sh...]
    pallas_call x1, Pallas kernels: 154 us -> 144 us  [step(): pl.pallas_call(functools.partial(step_kernel, sections, tensors, count, p...]
    pallas_call x1, Pallas kernels: 18.8 us -> 14.6 us  [update(): pl.pallas_call(functools.partial(update_kernel, pack, size), out_shape=(j...]
where the time goes in v4:
time: 223 us; the launch traced here: 222 us
  Pallas kernels  221 us (99%)
    pallas_call x1, Pallas kernels, step(): pl.pallas_call(functools.partial(step_kernel, sections, tensors, count, p...  144 us
    pallas_call x1, Pallas kernels, head(): pl.pallas_call(functools.partial(head_kernel, tensors, pack, per), out_sh...  62.4 us
    pallas_call x1, Pallas kernels, update(): pl.pallas_call(functools.partial(update_kernel, pack, size), out_shape=(j...  14.6 us

profile of v4, /device:TPU:1, one launch (start us, length us, event | category | flops | bytes accessed | tf_op | source)
XLA Modules:
  0.0 222.5 jit_solution(14597086701291036633)
XLA Ops:
  0.6 0.0 copy-start
  0.6 62.4 %shard_map.110 = (bf16[64,1664]{1,0:T(8,128)(2,1)}, f32[8,128]{1,0:T(8,128)}) custom-call(bf16[832,512]{1,0:T(8,128)(2,1)} %bitcast.17, s32[1,512]{1,0:T(1,128)} %bitcast.19, bf16[4000,6656]{1,0:T(8,128)(2,1)} %bitcast.13), custom_call_target="tpu_custom_call" | custom-call | tf_op jit(solution)/shard_map/pallas_call | solution.py:310
  63.1 0.0 copy-done
  63.1 1.0 copy.12.row_ref
  64.0 143.6 %shard_map.111 = (bf16[256,1664]{1,0:T(8,128)(2,1)}, bf16[832,6656]{1,0:T(8,128)(2,1)}, f32[8,128]{1,0:T(8,128)}, f32[832,1]{1,0:T(8,128)}, f32[832,1]{1,0:T(8,1...) custom-call(bf16[64,1664]{1,0:T(8,128)(2,1)} %get-tuple-element.19.part_ref, f32[8,128]{1,0:T(8,128)} %get-tuple-element.20.loss_ref, ...), custom_call_target="tpu_custom_call" | custom-call | tf_op jit(solution)/shard_map/pallas_call | solution.py:820
  207.7 14.6 %shard_map.112 = (bf16[832,6656]{1,0:T(8,128)(2,1)}, bf16[832,512]{1,0:T(8,128)(2,1)}, f32[1,832]{1,0:T(1,128)}, f32[1,6656]{1,0:T(1,128)}, f32[1,1]{1,0:T(1,128)}) custom-call(f32[832,1]{1,0:T(8,128)} %get-tuple-element.21.scale_ref, f32[1,6656]{1,0:T(1,128)} %get-tuple-element.22.col_ref, bf16[256,1664]{1,0:T(8,128)(2,1)} %get-tuple-element.23.carried_ref, ...), custom_call_target="tpu_custom_call" | custom-call | tf_op jit(solution)/shard_map/pallas_call | solution.py:791
Async XLA Ops:
  0.6 62.4 %copy-start = (f32[1,832]{1,0:T(1,128)S(1)}, f32[1,832]{1,0:T(1,128)}, u32[]{:S(2)}) copy-start(f32[1,832]{1,0:T(1,128)} %param.12) | copy-start | bytes 9988

commit v5 on v4

--- a/solution.py
+++ b/solution.py
@@ -34,9 +34,9 @@
 
 def head_kernel(
     tensors, pack, per, hidden_ref, labels_ref, w_ref, part_ref, loss_ref,
-    weight, tokens_ref, logits, slopes, mine, near_out, near, far_out, far, own_sums, sums,
+    weight, tokens_ref, logits, slopes, mine, near_out, near, far_out, far, relay, own_sums, sums,
     weight_sem, send_line, recv_line, send_mate, recv_mate, send_sum, recv_sum,
-    send_near, recv_near, send_far, recv_far, local_sem,
+    send_near, recv_near, send_far, recv_far, recv_relay, local_sem,
 ):
     section = lax.axis_index("section")
     me = lax.axis_index("tensor")
@@ -235,8 +235,24 @@
         first = core == 0
         return jnp.where(first, left, right), jnp.where(first, right, left)
 
+    relayed = chips == 4
+    low = chip < 2
+    neighbour = jnp.where(low, 1 - chip, 5 - chip)
+    across = 3 - chip
+
     def target_of(index):
-        return lax.rem(chip + 1 + index, chips)
+        if not relayed:
+            return lax.rem(chip + 1 + index, chips)
+        end_order = jnp.where(low, 3 - index, index)
+        far_end = jnp.where(low, 4 - index, index - 1)
+        middle_order = jnp.where(index == 0, neighbour, jnp.where(index == 3, chip, far_end))
+        return jnp.where(is_end, end_order, middle_order)
+
+    def relay_copy(index):
+        there = target_of(index)
+        return remote(
+            far_out.at[there], relay.at[index], send_far.at[there], recv_relay.at[index], neighbour * 2 + core
+        )
 
     def pair_sum(index):
         there = target_of(index)
@@ -253,15 +269,39 @@
         @pl.when(index > 0)
         def _():
             before = target_of(index - 1)
-            far_out[before] = pair_sum(index - 1).astype(far_out.dtype)
-            far_copy(chip, before).start()
+            if not relayed:
+                far_out[before] = pair_sum(index - 1).astype(far_out.dtype)
+                far_copy(chip, before).start()
+            else:
+                total = pair_sum(index - 1)
+                slot = jnp.clip(index - 2, 0, 1)
+
+                @pl.when(is_end | (index == 1))
+                def _():
+                    far_out[before] = total.astype(far_out.dtype)
+
+                @pl.when(jnp.logical_not(is_end) & (index > 1))
+                def _():
+                    relay_copy(slot).wait_recv()
+                    far_out[before] = (total + relay[slot].astype(jnp.float32)).astype(far_out.dtype)
+
+                @pl.when(is_end & (index < 3))
+                def _():
+                    relay_copy(jnp.minimum(index - 1, 1)).start()
+
+                @pl.when(jnp.logical_not(is_end) | (index == 3))
+                def _():
+                    far_copy(chip, before).start()
 
         return carry
 
     lax.fori_loop(0, chips, scatter_step, 0)
     result = pair_sum(chips - 1)
     chips_out = [lax.rem(chip + step, chips) for step in range(1, chips)]
-    for there in chips_out:
+    sources = chips_out
+    if relayed:
+        sources = [jnp.where(is_end, 1, neighbour), jnp.where(is_end, 2, across)]
+    for there in sources:
         far_copy(there, there).wait_recv()
         result = result + far[there].astype(jnp.float32)
     part_ref[...] = result.astype(part_ref.dtype)
@@ -291,8 +331,20 @@
         sum_copy(me, other).wait_send()
     for there in chips_out + [chip]:
         near_copy(there).wait_send()
-    for there in chips_out:
-        far_copy(chip, there).wait_send()
+    if not relayed:
+        for there in chips_out:
+            far_copy(chip, there).wait_send()
+    else:
+        @pl.when(is_end)
+        def _():
+            relay_copy(0).wait_send()
+            relay_copy(1).wait_send()
+            far_copy(chip, neighbour).wait_send()
+
+        @pl.when(jnp.logical_not(is_end))
+        def _():
+            for index in range(3):
+                far_copy(chip, target_of(index)).wait_send()
 
 
 def head(hidden, labels, head_weight, pack, per):
@@ -322,6 +374,7 @@
             pltpu.VMEM((share, vocab), jnp.bfloat16),
             pltpu.VMEM((2,) + dense, jnp.float32),
             held, held, held, held,
+            pltpu.VMEM((2,) + dense, jnp.bfloat16),
             pltpu.VMEM((8, share), jnp.float32),
             pltpu.VMEM((tensors, 8, share), jnp.float32),
             dma((groups,)),
@@ -335,6 +388,7 @@
             dma((chips,)),
             dma((chips,)),
             dma((chips,)),
+            dma((2,)),
             dma((1,)),
         ],
         compiler_params=pltpu.CompilerParams(
@@ -605,7 +659,8 @@
 
     lax.fori_loop(0, used, gather_squares, 0)
     sums = jnp.sum(row_acc[...], axis=1, keepdims=True)
-    fresh_row = decay_rate * row_ref[...] + (1.0 - decay_rate) * (sums / width)
+    old_row = jnp.broadcast_to(row_ref[...], (128, features)).T[:, :1]
+    fresh_row = decay_rate * old_row + (1.0 - decay_rate) * (sums / width)
     row_out[...] = fresh_row
     vectors[1, pl.ds(used, 1), :] = jnp.broadcast_to(jnp.sum(fresh_row, keepdims=True), (1, group))
     row_full[...] = jnp.broadcast_to(1.0 / fresh_row, row_full.shape)
@@ -876,7 +931,7 @@
     pack = 2 if (2 * features) % 128 == 0 and (size // 2) % 16 == 0 else 1
     part, losses = head(hidden_last.T, labels.reshape(1, -1), head_weight.T, pack, count // sections)
     new_weight, outputs, row_new, col_new, loss = step(
-        part, losses, layer_inputs[0].T, weights[0], row_state.reshape(-1, 1), col_state, pack, count
+        part, losses, layer_inputs[0].T, weights[0], row_state, col_state, pack, count
     )
     return (loss[0, 0], outputs.T[None], new_weight[None], row_new, col_new)
 

time: 223 us -> 218 us (0.978)
  Pallas kernels: 221 us -> 217 us
    pallas_call x1, Pallas kernels: 62.4 us -> 57.5 us  [head(): pl.pallas_call(functools.partial(head_kernel, tensors, pack, per), out_sh...]
where the time goes in v5:
time: 218 us
  Pallas kernels  217 us (100%)
    pallas_call x1, Pallas kernels, step(): pl.pallas_call(functools.partial(step_kernel, sections, tensors, count, p...  145 us
    pallas_call x1, Pallas kernels, head(): pl.pallas_call(functools.partial(head_kernel, tensors, pack, per), out_sh...  57.5 us
    pallas_call x1, Pallas kernels, update(): pl.pallas_call(functools.partial(update_kernel, pack, size), out_shape=(j...  14.6 us

profile of v5, /device:TPU:1, one launch (start us, length us, event | category | flops | bytes accessed | tf_op | source)
XLA Modules:
  0.0 217.8 jit_solution(13779945897262555640)
XLA Ops:
  0.6 57.5 %shard_map.110 = (bf16[64,1664]{1,0:T(8,128)(2,1)}, f32[8,128]{1,0:T(8,128)}) custom-call(bf16[832,512]{1,0:T(8,128)(2,1)} %bitcast.16, s32[1,512]{1,0:T(1,128)} %bitcast.17, bf16[4000,6656]{1,0:T(8,128)(2,1)} %bitcast.12), custom_call_target="tpu_custom_call" | custom-call | tf_op jit(solution)/shard_map/pallas_call | solution.py:362
  58.2 144.8 %shard_map.111 = (bf16[256,1664]{1,0:T(8,128)(2,1)}, bf16[832,6656]{1,0:T(8,128)(2,1)}, f32[8,128]{1,0:T(8,128)}, f32[832,1]{1,0:T(8,128)}, f32[832,1]{1,0:T(8,1...) custom-call(bf16[64,1664]{1,0:T(8,128)(2,1)} %get-tuple-element.19.part_ref, f32[8,128]{1,0:T(8,128)} %get-tuple-element.20.loss_ref, ...), custom_call_target="tpu_custom_call" | custom-call | tf_op jit(solution)/shard_map/pallas_call | solution.py:875
  203.0 14.6 %shard_map.112 = (bf16[832,6656]{1,0:T(8,128)(2,1)}, bf16[832,512]{1,0:T(8,128)(2,1)}, f32[1,832]{1,0:T(1,128)}, f32[1,6656]{1,0:T(1,128)}, f32[1,1]{1,0:T(1,128)}) custom-call(f32[832,1]{1,0:T(8,128)} %get-tuple-element.21.scale_ref, f32[1,6656]{1,0:T(1,128)} %get-tuple-element.22.col_ref, bf16[256,1664]{1,0:T(8,128)(2,1)} %get-tuple-element.23.carried_ref, ...), custom_call_target="tpu_custom_call" | custom-call | tf_op jit(solution)/shard_map/pallas_call | solution.py:846

commit v6 on v5

--- a/solution.py
+++ b/solution.py
@@ -658,6 +658,31 @@
         return carry
 
     lax.fori_loop(0, used, gather_squares, 0)
+
+    def mate_sum():
+        return remote(vectors.at[1 - core], near, send_sum.at[0], recv_sum.at[0], {"tensor": mate})
+
+    def far_sum(source, there):
+        return remote(
+            pair_sum, spread.at[source], send_far.at[there], recv_far.at[source], {"tensor": there * 2 + core}
+        )
+
+    def mate_total(side):
+        return remote(final.at[side], final.at[side], send_sum.at[1], recv_sum.at[1], {"tensor": mate})
+
+    others = [rem(chip + step, chips) for step in range(1, chips)]
+
+    def spread_pair():
+        mate_sum().wait_recv()
+        pair_sum[...] = vectors[core] + near[...]
+        for there in others:
+            far_sum(chip, there).start()
+        spread[chip] = pair_sum[...]
+
+    @pl.when(core == 1)
+    def _():
+        mate_sum().start()
+
     sums = jnp.sum(row_acc[...], axis=1, keepdims=True)
     old_row = jnp.broadcast_to(row_ref[...], (128, features)).T[:, :1]
     fresh_row = decay_rate * old_row + (1.0 - decay_rate) * (sums / width)
@@ -675,26 +700,20 @@
         vectors[1, pl.ds(index, 1), :] = jnp.sum(inner, axis=0, keepdims=True)
         return carry
 
+    @pl.when(core == 0)
+    def _():
+        spread_pair()
+
     lax.fori_loop(0, used, gather_scaled, 0)
 
-    def mate_sum():
-        return remote(vectors.at[1 - core], near, send_sum.at[0], recv_sum.at[0], {"tensor": mate})
-
-    def far_sum(source, there):
-        return remote(
-            pair_sum, spread.at[source], send_far.at[there], recv_far.at[source], {"tensor": there * 2 + core}
-        )
-
-    def mate_total(side):
-        return remote(final.at[side], final.at[side], send_sum.at[1], recv_sum.at[1], {"tensor": mate})
-
-    others = [rem(chip + step, chips) for step in range(1, chips)]
-    mate_sum().start()
-    mate_sum().wait_recv()
-    pair_sum[...] = vectors[core] + near[...]
-    for there in others:
-        far_sum(chip, there).start()
-    spread[chip] = pair_sum[...]
+    @pl.when(core == 0)
+    def _():
+        mate_sum().start()
+
+    @pl.when(core == 1)
+    def _():
+        spread_pair()
+
     for there in others:
         far_sum(there, there).wait_recv()
     final[core] = jnp.sum(spread[...], axis=0)

time: 218 us -> 217 us (level)
  no operation moved by 1% of the time
where the time goes in v6:
time: 217 us; the launch traced here: 216 us
  Pallas kernels  215 us (99%)
    pallas_call x1, Pallas kernels, step(): pl.pallas_call(functools.partial(step_kernel, sections, tensors, count, p...  143 us
    pallas_call x1, Pallas kernels, head(): pl.pallas_call(functools.partial(head_kernel, tensors, pack, per), out_sh...  57.5 us
    pallas_call x1, Pallas kernels, update(): pl.pallas_call(functools.partial(update_kernel, pack, size), out_shape=(j...  14.6 us

profile of v6, /device:TPU:1, one launch (start us, length us, event | category | flops | bytes accessed | tf_op | source)
XLA Modules:
  0.0 215.7 jit_solution(3309497977272357315)
XLA Ops:
  0.6 57.5 %shard_map.110 = (bf16[64,1664]{1,0:T(8,128)(2,1)}, f32[8,128]{1,0:T(8,128)}) custom-call(bf16[832,512]{1,0:T(8,128)(2,1)} %bitcast.16, s32[1,512]{1,0:T(1,128)} %bitcast.17, bf16[4000,6656]{1,0:T(8,128)(2,1)} %bitcast.12), custom_call_target="tpu_custom_call" | custom-call | tf_op jit(solution)/shard_map/pallas_call | solution.py:362
  58.2 142.9 %shard_map.111 = (bf16[256,1664]{1,0:T(8,128)(2,1)}, bf16[832,6656]{1,0:T(8,128)(2,1)}, f32[8,128]{1,0:T(8,128)}, f32[832,1]{1,0:T(8,128)}, f32[832,1]{1,0:T(8,1...) custom-call(bf16[64,1664]{1,0:T(8,128)(2,1)} %get-tuple-element.19.part_ref, f32[8,128]{1,0:T(8,128)} %get-tuple-element.20.loss_ref, ...), custom_call_target="tpu_custom_call" | custom-call | tf_op jit(solution)/shard_map/pallas_call | solution.py:894
  201.1 14.6 %shard_map.112 = (bf16[832,6656]{1,0:T(8,128)(2,1)}, bf16[832,512]{1,0:T(8,128)(2,1)}, f32[1,832]{1,0:T(1,128)}, f32[1,6656]{1,0:T(1,128)}, f32[1,1]{1,0:T(1,128)}) custom-call(f32[832,1]{1,0:T(8,128)} %get-tuple-element.21.scale_ref, f32[1,6656]{1,0:T(1,128)} %get-tuple-element.22.col_ref, bf16[256,1664]{1,0:T(8,128)(2,1)} %get-tuple-element.23.carried_ref, ...), custom_call_target="tpu_custom_call" | custom-call | tf_op jit(solution)/shard_map/pallas_call | solution.py:865
